TPU v7x, 512 devices: a whole 4x4x16 slice. The times are simulated.
512 devices in a mesh: slab: 8 (over z_hi, core), vel: 64 (over x, y, z_lo).
Axes of the slice: x: 4, y: 4, z: 16 (z_hi: 4, z_lo: 4; z = z_hi * 4 + z_lo), core: 2. Of those that a mesh axis runs over, the one named last changes fastest.
Arguments:
- f_start: float32 [4096, 8, 8, 128], P('vel', 'slab'), as said below
- links: int32 [3, 8, 8, 128], P(None, 'slab'), may hold values 0 or 1
- solid: int32 [8, 8, 128], P('slab'), may hold values 0 or 1
Outputs:
- f_final: float32 [4096, 8, 8, 128], P('vel', 'slab')
Inputs may be any that keep to these rules, and one draw needn't show every extreme that they name: `f_start`: every entry is positive.
All inputs are finite; a program needn't handle non-finite values. No bound on the sum of `links` or of `solid` on one device may be relied on, other than what follows from the above.
Results may differ from a plain program's by a relative error of at most 0.0003.
Values sent between devices are 32-bit elements; how exact they have to be, the bound alone decides.
No kernel may reach another device: no remote copies, remote signals or barrier semaphores. Data moves between devices by JAX's collectives and lax.ppermute only.
A program may use at most 64 MiB of HBM per device.

v0:
```python
import math

import jax
import jax.numpy as jnp
from jax import lax
from jax.sharding import PartitionSpec as P

NQ = 16
STEPS = 2
SWEEPS = 2


SPACING = 0.6
COUPLING = 1.0
COURANT = 0.06
RELAXATION_FREQ = 0.5
VISCOUS_TO_HEAT = 2.0 / 3.0
QUAD_WEIGHT = SPACING**3 / (2.0 * math.pi) ** 1.5


def passed_along(block, axis, distance):
    devices = range(lax.axis_size(axis))
    route = [(i - distance, i) for i in devices if i - distance in devices]
    return lax.ppermute(block, axis, route)


def padded_2(cells, sides, width):
    for axis, dim in sides:
        count = lax.axis_size(axis)
        ends = count - 1
        head = lax.slice_in_dim(cells, 0, width, axis=dim)
        tail = lax.slice_in_dim(cells, cells.shape[dim] - width, cells.shape[dim], axis=dim)
        cells = jnp.concatenate(
            [
                lax.ppermute(tail, axis, [(i, (i + 1) % count) for i in range(ends)]),
                cells,
                lax.ppermute(head, axis, [((i + 1) % count, i) for i in range(ends)]),
            ],
            axis=dim,
        )
    return cells


def lattice_of(first, number):
    index = first + lax.iota(jnp.int32, number)
    comp_x = index % NQ
    comp_y = index // NQ % NQ
    comp_z = index // (NQ * NQ)
    stacked = jnp.stack([comp_x, comp_y, comp_z]).astype(jnp.float32)
    return (stacked - (NQ - 1) / 2.0) * SPACING


def moment_basis(lattice):
    overall_work_content = 0.5 * jnp.sum(lattice * lattice, axis=0)
    rows = [
        jnp.ones_like(overall_work_content),
        lattice[0],
        lattice[1],
        lattice[2],
        overall_work_content,
        lattice[0] * overall_work_content,
        lattice[1] * overall_work_content,
        lattice[2] * overall_work_content,
    ]
    return jnp.stack(rows) * QUAD_WEIGHT


def shift_down(values, axis_dim):
    pads = [(0, 0)] * values.ndim
    pads[axis_dim] = (1, 0)
    return lax.slice_in_dim(jnp.pad(values, pads), 0, values.shape[axis_dim], axis=axis_dim)


def shift_up(values, axis_dim):
    pads = [(0, 0)] * values.ndim
    pads[axis_dim] = (0, 1)
    return lax.slice_in_dim(jnp.pad(values, pads), 1, values.shape[axis_dim] + 1, axis=axis_dim)


def macro_state(predicted):
    matter_per_volume = predicted[0]
    mean_flow_vector = predicted[1:4] / matter_per_volume
    overall_work_content = predicted[4]
    fluid_hotness_level = (
        2.0 * overall_work_content / matter_per_volume
        - jnp.sum(mean_flow_vector * mean_flow_vector, axis=0)
    ) / 3.0
    fluid_normal_stress = matter_per_volume * fluid_hotness_level
    heat_current_vector = predicted[5:8] - mean_flow_vector * (
        overall_work_content + fluid_normal_stress
    )
    relaxation_update = RELAXATION_FREQ * matter_per_volume * fluid_hotness_level**0.28
    profile_multiplier = (
        (1.0 - VISCOUS_TO_HEAT)
        * heat_current_vector
        / (5.0 * fluid_normal_stress * fluid_hotness_level)
    )
    perturbation_height = matter_per_volume * fluid_hotness_level ** (-1.5)
    return (
        mean_flow_vector,
        fluid_hotness_level,
        relaxation_update,
        profile_multiplier,
        perturbation_height,
    )


def upwind_local(dist, speed, axis_dim):
    return jnp.where(speed > 0, shift_down(dist, axis_dim), shift_up(dist, axis_dim))


def transport(dist, upwind_x, lattice, particle_population, open_up, open_low, solid):
    (
        mean_flow_vector,
        fluid_hotness_level,
        relaxation_update,
        profile_multiplier,
        perturbation_height,
    ) = particle_population
    peculiar = lattice[:, :, None, None, None] - mean_flow_vector[:, None]
    acoustic_celerity_power = jnp.sum(peculiar * peculiar, axis=0)
    matching_arrangement = jnp.sum(peculiar * profile_multiplier[:, None], axis=0)
    relaxed_distribution_goal = (
        perturbation_height
        * jnp.exp(-acoustic_celerity_power / (2.0 * fluid_hotness_level))
        * (1.0 + matching_arrangement * (acoustic_celerity_power / fluid_hotness_level - 5.0))
    )
    flux = jnp.zeros_like(dist)
    for axis_dim in range(3):
        speed = lattice[axis_dim][:, None, None, None]
        rising = speed > 0
        outward = jnp.where(rising, open_up[axis_dim], open_low[axis_dim])
        inward = jnp.where(rising, open_low[axis_dim], open_up[axis_dim])
        if axis_dim == 0:
            neighbour = upwind_x
        else:
            neighbour = upwind_local(dist, speed, axis_dim + 1)
        flux = flux + jnp.abs(speed) * (outward * dist - inward * neighbour)
    fresh = (dist - COURANT * flux + relaxation_update * relaxed_distribution_goal) / (
        1.0 + relaxation_update
    )
    return jnp.where(solid > 0, dist, fresh)


def relax(moments, padded, open_up, open_low, count):
    center = padded[:, 1:-1, :, 1:-1]
    beside_all = (
        padded[:, 2:, :, 1:-1] * open_up[0]
        + padded[:, :-2, :, 1:-1] * open_low[0]
        + shift_up(center, 2) * open_up[1]
        + shift_down(center, 2) * open_low[1]
        + padded[:, 1:-1, :, 2:] * open_up[2]
        + padded[:, 1:-1, :, :-2] * open_low[2]
    )
    return (moments + COUPLING * beside_all) / (1.0 + COUPLING * count)


def body(f_start, links, solid):
    vel_local = f_start.shape[0]
    rank = lax.axis_index("vel")
    width_z = f_start.shape[3]
    block_z = width_z // lax.axis_size("vel")
    lattice = lattice_of(rank * vel_local, vel_local)
    basis = moment_basis(lattice)
    open_up = links.astype(jnp.float32)
    plane = passed_along(links[0, -1:], "slab", 1)
    low_x = jnp.concatenate([plane, links[0, :-1]], axis=0).astype(jnp.float32)
    open_low = jnp.stack([low_x, shift_down(open_up[1], 1), shift_down(open_up[2], 2)])
    count = jnp.sum(open_up, axis=0) + jnp.sum(open_low, axis=0)
    start_z = rank * block_z
    part_up = lax.dynamic_slice_in_dim(open_up, start_z, block_z, axis=3)
    part_low = lax.dynamic_slice_in_dim(open_low, start_z, block_z, axis=3)
    part_count = lax.dynamic_slice_in_dim(count, start_z, block_z, axis=2)
    dist = f_start
    for repeat in range(STEPS):
        partial_value = jnp.dot(basis, dist.reshape(vel_local, -1), precision=lax.Precision.HIGHEST)
        partial_value = partial_value.reshape((8,) + dist.shape[1:])
        moments = lax.psum_scatter(partial_value, "vel", scatter_dimension=3, tiled=True)
        predicted = moments
        for sweeping in range(SWEEPS):
            padded = padded_2(predicted, (("slab", 1), ("vel", 3)), 1)
            predicted = relax(moments, padded, part_up, part_low, part_count)
        predicted = lax.all_gather(predicted, "vel", axis=3, tiled=True)
        particle_population = macro_state(predicted)
        extended = padded_2(dist, (("slab", 1),), 1)
        speed = lattice[0][:, None, None, None]
        upwind_x = jnp.where(speed > 0, extended[:, :-2], extended[:, 2:])
        dist = transport(dist, upwind_x, lattice, particle_population, open_up, open_low, solid)
    return dist


def solution(mesh):
    in_specs = (P("vel", "slab", None, None), P(None, "slab", None, None), P("slab", None, None))
    out_specs = P("vel", "slab", None, None)
    return jax.shard_map(body, mesh=mesh, in_specs=in_specs, out_specs=out_specs, check_vma=False)
```

profile of v0, /device:TPU:128, one launch (start us, length us, event | category | flops | bytes accessed | tf_op | source)
XLA Modules:
  0.0 1251.2 jit_solution(8201192612904787884)
XLA Ops:
  6.5 1.9 collective-permute-start.1
  8.5 7.6 collective-permute-start.2
  19.1 3.6 collective-permute-start
  23.0 4.9 collective-permute-done
  28.1 374.6 %reduce-scatter.3.cloned.1.call-done = f32[8,1,8,2]{2,0,1,3:T(8,128)} async-done(((f32[8,1,8,128]{2,0,1,3:T(8,128)}), f32[8,1,8,2]{2,0,1,3:T(8,128)}) %reduce-scatter.3.cloned.1.call-update) | async-done | bytes 528 | tf_op jit(solution)/shard_map/reduce_scatter | solution.py:178
  402.7 1.9 collective-permute-start.4
  404.6 7.5 collective-permute-start.3
  412.2 1.5 collective-permute-done.3
  413.8 1.3 collective-permute-start.5
  415.1 4.5 collective-permute-start.6
  421.1 4.7 collective-permute-start.8
  425.8 4.7 collective-permute-start.7
  430.6 1.3 collective-permute-done.7
  431.9 4.2 collective-permute-start.10
  436.1 1.3 collective-permute-start.9
  437.5 4.2 collective-permute-done.9
  441.8 182.9 %all_gather.6 = f32[8,1,8,128]{2,0,1,3:T(8,128)S(1)} all-gather(f32[8,1,8,2]{2,0,1,3:T(8,128)S(1)} %fusion.79), channel_id=1, replica_groups=mesh['slab'=8,'vel'=64] {'vel'}, dimensions={3}, use_global_device_ids=true | all-gather | bytes 33280 | tf_op jit(solution)/shard_map/all_gather | solution.py:183
  629.5 377.2 %reduce-scatter.5.cloned.1.call-done = f32[8,1,8,2]{2,0,1,3:T(8,128)} async-done(((f32[8,1,8,128]{2,0,1,3:T(8,128)}), f32[8,1,8,2]{2,0,1,3:T(8,128)}) %reduce-scatter.5.cloned.1.call-update) | async-done | bytes 528 | tf_op jit(solution)/shard_map/reduce_scatter | solution.py:178
  1006.7 1.9 collective-permute-start.14
  1008.6 7.5 collective-permute-start.13
  1016.2 1.5 collective-permute-done.13
  1018.4 1.3 collective-permute-start.15
  1019.7 4.5 collective-permute-start.16
  1024.3 1.4 collective-permute-done.16
  1025.7 4.0 collective-permute-start.18
  1029.7 5.5 collective-permute-start.17
  1035.2 1.3 collective-permute-done.17
  1037.9 4.8 collective-permute-start.20
  1042.7 4.7 collective-permute-start.11
  1047.5 4.7 collective-permute-start.12
  1052.3 188.5 %all_gather.7 = f32[8,1,8,128]{2,0,1,3:T(8,128)S(1)} all-gather(f32[8,1,8,2]{2,0,1,3:T(8,128)S(1)} %fusion.63), channel_id=1, replica_groups=mesh['slab'=8,'vel'=64] {'vel'}, dimensions={3}, use_global_device_ids=true | all-gather | bytes 33280 | tf_op jit(solution)/shard_map/all_gather | solution.py:183
  1242.9 1.5 fusion.58
  (98 shorter events, 14.2 us)
Async XLA Ops:
  6.5 396.2 %reduce-scatter.3.cloned.1.call-start = ((), (), s32[]{:S(2)}) async-start(), calls=%async_computation.2 | async-start | bytes 532480 | tf_op jit(solution)/shard_map/reduce_scatter | solution.py:178
  6.5 620.2 %collective-permute-start.1 = (f32[64,1,8,128]{3,2,0,1:T(8,128)}, f32[64,1,8,128]{3,2,0,1:T(8,128)S(1)}, u32[]{:S(2)}, u32[]{:S(2)}) collective-permute-start(f32[64,1,8,128]{3,2,0,1:T(8,128)} %bitcast.271), channel_id=1, source_target_pairs={{0,64},{64,128},{128,192},{192,256},{256,320},{320,384},{384,448},... | collective-permute-start | bytes 786440 | tf_op jit(solution)/shard_map/ppermute | solution.py:35
  8.5 618.3 %collective-permute-start.2 = (f32[64,1,8,128]{3,2,0,1:T(8,128)}, f32[64,1,8,128]{3,2,0,1:T(8,128)S(1)}, u32[]{:S(2)}, u32[]{:S(2)}) collective-permute-start(f32[64,1,8,128]{3,2,0,1:T(8,128)} %bitcast.272), channel_id=1, source_target_pairs={{64,0},{128,64},{192,128},{256,192},{320,256},{384,320},{448,384},... | collective-permute-start | bytes 786440 | tf_op jit(solution)/shard_map/ppermute | solution.py:37
  18.4 0.7 copy-start.3
  18.4 988.3 %reduce-scatter.5.cloned.1.call-start = ((), (), s32[]{:S(2)}) async-start(), calls=%async_computation.3 | async-start | bytes 532480 | tf_op jit(solution)/shard_map/reduce_scatter | solution.py:178
  19.1 8.8 collective-permute-start
  402.7 9.5 collective-permute-start.4
  404.6 9.1 collective-permute-start.3
  412.2 1.6 copy-start.1
  413.8 6.3 collective-permute-start.5
  415.1 5.9 collective-permute-start.6
  421.0 9.6 copy-start.4
  421.1 9.5 collective-permute-start.8
  425.8 6.1 collective-permute-start.7
  431.9 5.6 collective-permute-start.10
  436.1 5.6 collective-permute-start.9
  626.4 1.0 copy-start
  1006.7 9.5 collective-permute-start.14
  1008.6 9.1 collective-permute-start.13
  1018.4 7.3 copy-start.2
  1018.4 5.9 collective-permute-start.15
  1019.7 5.9 collective-permute-start.16
  1025.7 9.5 collective-permute-start.18
  1029.7 6.8 collective-permute-start.17
  1036.6 15.6 %collective-permute-start.19 = (f32[8,3,8,1]{2,0,3,1:T(8,128)S(1)}, f32[8,3,8,1]{2,0,3,1:T(8,128)S(1)}, u32[]{:S(2)}, u32[]{:S(2)}) collective-permute-start(f32[8,3,8,1]{2,0,3,1:T(8,128)S(1)} %get-tuple-element.29), channel_id=1, source_target_pairs={{1,0},{2,1},{3,2},{4,3},{5,4},{6,5},{7,6},{8,7},{9,8},{10,9},{11,1... | collective-permute-start | bytes 2312 | tf_op jit(solution)/shard_map/ppermute | solution.py:37
  1037.9 14.3 %collective-permute-start.20 = (f32[8,3,8,1]{2,0,3,1:T(8,128)S(1)}, f32[8,3,8,1]{2,0,3,1:T(8,128)S(1)}, u32[]{:S(2)}, u32[]{:S(2)}) collective-permute-start(f32[8,3,8,1]{2,0,3,1:T(8,128)S(1)} %get-tuple-element.30), channel_id=1, source_target_pairs={{0,1},{1,2},{2,3},{3,4},{4,5},{5,6},{6,7},{7,8},{8,9},{9,10},{10,1... | collective-permute-start | bytes 2312 | tf_op jit(solution)/shard_map/ppermute | solution.py:35
  1042.7 200.2 %collective-permute-start.11 = (f32[64,1,8,128]{3,2,0,1:T(8,128)S(1)}, f32[64,1,8,128]{3,2,0,1:T(8,128)S(1)}, u32[]{:S(2)}, u32[]{:S(2)}) collective-permute-start(f32[64,1,8,128]{3,2,0,1:T(8,128)S(1)} %fusion.12), channel_id=1, source_target_pairs={{0,64},{64,128},{128,192},{192,256},{256,320},{320,384},{384,448},... | collective-permute-start | bytes 786440 | tf_op jit(solution)/shard_map/ppermute | solution.py:35
  1047.5 195.4 %collective-permute-start.12 = (f32[64,1,8,128]{3,2,0,1:T(8,128)S(1)}, f32[64,1,8,128]{3,2,0,1:T(8,128)S(1)}, u32[]{:S(2)}, u32[]{:S(2)}) collective-permute-start(f32[64,1,8,128]{3,2,0,1:T(8,128)S(1)} %fusion.12), channel_id=1, source_target_pairs={{64,0},{128,64},{192,128},{256,192},{320,256},{384,320},{448,384},... | collective-permute-start | bytes 786440 | tf_op jit(solution)/shard_map/ppermute | solution.py:37
Sparse Core Ops, SparseCore 0:
  18.5 384.1 reduce-scatter.2
  629.6 376.9 reduce-scatter.4
where the time goes:
time: 1250 us
  waiting for transfers between devices  769 us (62%)
  blocking collectives  371 us (30%)
  starting transfers between devices  83.7 us (7%)
  between operations  13.9 us (1%)
    reduce_scatter x2, waiting for transfers between devices, body(): lax.psum_scatter(partial_value, 'vel', scatter_dimension=3, tiled=True)  752 us
    all_gather x2, blocking collectives, body(): predicted = lax.all_gather(predicted, 'vel', axis=3, tiled=True)  371 us
    ppermute x10, starting transfers between devices, padded_2(): lax.ppermute(head, axis, [((i + 1) % count, i) for i in range(ends)])  42.7 us
    ppermute x10, starting transfers between devices, padded_2(): lax.ppermute(tail, axis, [(i, (i + 1) % count) for i in range(ends)])  37.3 us
  transfers between devices with their start and end apart: 23, of which 11 were waited for; matrix products, arithmetic and copies ran while one was open for 1% of the time, Pallas kernels for 0%

commit v1 on v0

v1 whole, which is shorter than its diff:
```python
import math

import jax
import jax.numpy as jnp
from jax import lax
from jax.experimental import pallas as pl
from jax.experimental.pallas import tpu as pltpu
from jax.sharding import Mesh
from jax.sharding import PartitionSpec as P

NQ = 16
HALF = NQ // 2
LY = 4
NS = 8
NY, NZ = 8, 128
SPACING = 0.6
COURANT = 0.06
RELAXATION_FREQ = 0.5
VISCOUS_TO_HEAT = 2.0 / 3.0
QUAD_WEIGHT = SPACING**3 / (2.0 * math.pi) ** 1.5
F32 = jnp.float32

SLAB = ("zh", "core")
VEL = ("x", "y", "zl")


def rows_and_lanes():
    row = lax.broadcasted_iota(jnp.int32, (NY, NZ), 0)
    lane = lax.broadcasted_iota(jnp.int32, (NY, NZ), 1)
    return row, lane


def down(v, axis):
    return pltpu.roll(v, 1, axis)


def up(v, axis):
    return pltpu.roll(v, v.shape[axis] - 1, axis)


def speed_of(index):
    return (index.astype(F32) - (NQ - 1) / 2.0) * SPACING


def sides(links, axis, first, last, rising):
    open_up = links
    open_low = jnp.where(first, 0.0, down(links, axis))
    inner_up = jnp.where(last, 0.0, links)
    return jnp.where(rising, open_up, open_low), jnp.where(rising, open_low, inner_up)


def moments_kernel(place, f_ref, links_ref, out_ref):
    rank = place[0]
    row, lane = rows_and_lanes()
    zv = speed_of(rank // 4)
    z_rising, y_rising = rank // 4 >= HALF, rank % 4 >= 2
    ly = links_ref[1].astype(F32)
    lz = links_ref[2].astype(F32)
    out_y, in_y = sides(ly, 0, row == 0, row == NY - 1, y_rising)
    out_z, in_z = sides(lz, 1, lane == 0, lane == NZ - 1, z_rising)
    shift_y = jnp.where(y_rising, 1, NY - 1)
    shift_z = jnp.where(z_rising, 1, NZ - 1)
    az = COURANT * jnp.abs(zv)
    out_z, in_z = az * out_z, az * in_z
    totals = None
    for jy in range(LY):
        yv = speed_of(rank % 4 * LY + jy)
        ay = COURANT * jnp.abs(yv)
        pos, neg = [None] * 5, [None] * 5
        for j in range(HALF):
            a = (j + 0.5) * SPACING
            fp = f_ref[jy * NQ + HALF + j]
            fn = f_ref[jy * NQ + HALF - 1 - j]
            for n in range(5):
                wp = fp if n == 0 else fp * a**n
                wn = fn if n == 0 else fn * a**n
                pos[n] = wp if pos[n] is None else pos[n] + wp
                neg[n] = wn if neg[n] is None else neg[n] + wn
        full = [pos[n] + neg[n] if n % 2 == 0 else pos[n] - neg[n] for n in range(4)]
        keep = 1.0 - ay * out_y - out_z
        moved = [
            keep * v + (ay * in_y) * pltpu.roll(v, shift_y, 0) + in_z * pltpu.roll(v, shift_z, 1)
            for v in full
        ]
        plus = pos[1:5]
        minus = [neg[1], -neg[2], neg[3], -neg[4]]
        q = yv * yv + zv * zv
        parts = []
        for a0, a1, a2, a3 in (full, moved, plus, minus):
            e0 = 0.5 * (a2 + q * a0)
            e1 = 0.5 * (a3 + q * a1)
            parts.append([a0, a1, yv * a0, e0, e1, yv * e0])
        if totals is None:
            totals = parts
        else:
            totals = [[t + p for t, p in zip(ts, ps)] for ts, ps in zip(totals, parts)]
    for kind, (b0, b1, by, e0, e1, ey) in enumerate(totals):
        for k, v in enumerate((b0, b1, by, zv * b0, e0, e1, ey, zv * e0)):
            out_ref[pl.ds(k * 32 + kind, NY, stride=4), :] = v * QUAD_WEIGHT


def owner_kernel(place, parts_ref, links_ref, solid_ref, out_ref):
    rank = place[0]
    k, y = rank // 8, rank % 8
    total = parts_ref[0]
    for i in range(1, 32):
        total = total + parts_ref[i]
    total = total + pltpu.roll(total, 4, 0)
    row = lax.broadcasted_iota(jnp.int32, (8, NZ), 0)
    flags = [links_ref[a, pl.ds(y, 1), :].astype(F32) for a in range(3)]
    flags.append(solid_ref[pl.ds(y, 1), :].astype(F32))
    kind = k % 4
    own = jnp.where(kind == 0, flags[0], jnp.where(kind == 1, flags[1], jnp.where(kind == 2, flags[2], flags[3])))
    block = jnp.where(row < 4, total, jnp.where(row == 4, flags[0], jnp.where(row == 5, own, 0.0)))
    for i in range(out_ref.shape[0]):
        out_ref[i] = block


def combine_kernel(place, parts_ref, out_ref):
    rank = place[0]
    kinds = [parts_ref[pl.ds(kind, 32, stride=8), :] for kind in range(6)]
    m0, q, hp, hm, lx, own = kinds
    row = lax.broadcasted_iota(jnp.int32, (32, NZ), 0)
    low = jnp.where(row < 4, 0.0, pltpu.roll(lx, 4, 0))
    inner = jnp.where(row >= 28, 0.0, lx)
    mt = q - COURANT * (lx * hp + low * hm - low * pltpu.roll(hp, 4, 0) - inner * pltpu.roll(hm, 28, 0))
    half = jnp.where(rank // 32 == 0, own[:16], own[16:])
    for i in range(out_ref.shape[0]):
        out_ref[i, 0:32, :] = m0
        out_ref[i, 32:64, :] = mt
        out_ref[i, 64:80, :] = half


def macro_state(p):
    rho = p[0]
    inv = 1.0 / rho
    u = [p[1 + a] * inv for a in range(3)]
    energy = p[4]
    u2 = u[0] * u[0] + u[1] * u[1] + u[2] * u[2]
    temp = (2.0 * energy * inv - u2) / 3.0
    stress = rho * temp
    nu = RELAXATION_FREQ * rho * jnp.exp(0.28 * jnp.log(temp))
    scale = (1.0 - VISCOUS_TO_HEAT) / (5.0 * stress * temp)
    s = [(p[5 + a] - u[a] * (energy + stress)) * scale for a in range(3)]
    inv_t = 1.0 / temp
    height = rho * inv_t * lax.sqrt(inv_t)
    return u, u2, inv_t, nu, s, height


def xi(i):
    return (i - (NQ - 1) / 2.0) * SPACING


def target_moments(u, u2, inv_t, s, height):
    half_t = -0.5 * inv_t
    one_d = []
    for a in range(3):
        m = [None] * 7
        for i in range(NQ):
            c = xi(i) - u[a]
            t = jnp.exp(c * c * half_t)
            for n in range(7):
                m[n] = t if m[n] is None else m[n] + t
                if n < 6:
                    t = t * c
        one_d.append(m)
    x, y, z = one_d
    s5 = [-5.0 * v for v in s]
    st = [v * inv_t for v in s]
    cache = {}

    def xy(i, j):
        if (i, j) not in cache:
            cache[i, j] = x[i] * y[j]
        return cache[i, j]

    def plain(i, j, k):
        return xy(i, j) * z[k]

    def mean(i, j, k):
        total = plain(i, j, k)
        for a in range(3):
            e = [i, j, k]
            e[a] += 1
            square = None
            for b in range(3):
                d = list(e)
                d[b] += 2
                t = plain(*d)
                square = t if square is None else square + t
            total = total + s5[a] * plain(*e) + st[a] * square
        return total

    def unit(*axes):
        e = [0, 0, 0]
        for a in axes:
            e[a] += 1
        return mean(*e)

    n0 = unit()
    n1 = [unit(a) for a in range(3)]
    n2 = {(a, b): unit(a, b) for a in range(3) for b in range(a, 3)}
    n3 = [unit(a, 0, 0) + unit(a, 1, 1) + unit(a, 2, 2) for a in range(3)]
    weight = QUAD_WEIGHT * height
    j_e = 0.5 * (n2[0, 0] + n2[1, 1] + n2[2, 2] + u2 * n0) + u[0] * n1[0] + u[1] * n1[1] + u[2] * n1[2]
    rows = [n0] + [n1[a] + u[a] * n0 for a in range(3)] + [j_e]
    for a in range(3):
        cross = sum(u[b] * n2[min(a, b), max(a, b)] for b in range(3))
        rows.append(0.5 * (n3[a] + u2 * n1[a]) + cross + u[a] * j_e)
    return [weight * r for r in rows]


def neighbours(v, w):
    return w[2] * up(v, 0) + w[3] * down(v, 0) + w[4] * up(v, 1) + w[5] * down(v, 1)


def finish_kernel(
    place, got_ref, f_ref, p1_ref, p2_ref, n1_ref, n2_ref, out_ref, m_ref, l_ref, w_ref, pred_ref, next_ref,
    xe_ref, xc_ref, f1_ref, h1_ref,
):
    rank, slab = place[0], place[1]
    row, lane = rows_and_lanes()
    low_half = row < 4
    zero = jnp.zeros((NY, NZ), F32)

    for a in range(4):
        l_ref[a, 0] = zero
        l_ref[a, NS + 1] = zero

    @pl.loop(0, 8)
    def _(k):
        for t in range(10):
            t0, t1 = got_ref[2 * k, t], got_ref[2 * k + 1, t]
            first = jnp.where(low_half, t0, pltpu.roll(t1, 4, 0))
            second = jnp.where(low_half, pltpu.roll(t0, 4, 0), t1)
            if t < 8:
                m_ref[t // 4, k, 2 * (t % 4)] = first
                m_ref[t // 4, k, 2 * (t % 4) + 1] = second
            else:
                base = 1 + k // 4 * 4 + 2 * (t - 8)
                l_ref[k % 4, base] = first
                l_ref[k % 4, base + 1] = second

    for a in range(7):
        w_ref[a, 0] = zero
        w_ref[a, NS + 1] = zero
    for s in range(NS):
        lx, lx_low = l_ref[0, s + 1], l_ref[0, s]
        ly, lz = l_ref[1, s + 1], l_ref[2, s + 1]
        ly_low = jnp.where(row == 0, 0.0, down(ly, 0))
        lz_low = jnp.where(lane == 0, 0.0, down(lz, 1))
        share = 1.0 / (1.0 + (lx + ly + lz + lx_low + ly_low + lz_low))
        w_ref[0, s + 1] = share * lx if s < NS - 1 else zero
        w_ref[1, s + 1] = share * lx_low
        w_ref[2, s + 1] = jnp.where(row == NY - 1, 0.0, share * ly)
        w_ref[3, s + 1] = share * ly_low
        w_ref[4, s + 1] = jnp.where(lane == NZ - 1, 0.0, share * lz)
        w_ref[5, s + 1] = share * lz_low
        w_ref[6, s + 1] = share

    @pl.loop(0, 8)
    def _(k):
        start = [m_ref[0, k, s] for s in range(NS)]
        now = start
        for _ in range(2):
            new = []
            for s in range(NS):
                w = [w_ref[a, s + 1] for a in range(7)]
                v = w[6] * start[s] + neighbours(now[s], w)
                if s < NS - 1:
                    v = v + w[0] * now[s + 1]
                if s > 0:
                    v = v + w[1] * now[s - 1]
                new.append(v)
            now = new
        for s in range(NS):
            pred_ref[k, s] = now[s]

    for k in range(8):
        for i in (0, 1, NS + 2, NS + 3):
            next_ref[k, i] = zero

    @pl.loop(jnp.maximum(slab - 2, 0), jnp.minimum(slab + 3, NS))
    def _(w):
        u, u2, inv_t, nu, s, height = macro_state([pred_ref[k, w] for k in range(8)])
        goal = target_moments(u, u2, inv_t, s, height)
        body = l_ref[3, w + 1] > 0
        share = 1.0 / (1.0 + nu)
        for k in range(8):
            fresh = (m_ref[1, k, w] + nu * goal[k]) * share
            next_ref[k, w + 2] = jnp.where(body, m_ref[0, k, w], fresh)

    last = []
    for k in range(8):
        around = [next_ref[k, slab + i] for i in range(5)]
        mids = []
        for i in range(3):
            w = [w_ref[a, slab + i] for a in range(7)]
            mids.append(
                w[6] * around[i + 1] + w[0] * around[i + 2] + w[1] * around[i] + neighbours(around[i + 1], w)
            )
        w = [w_ref[a, slab + 1] for a in range(7)]
        last.append(w[6] * around[2] + w[0] * mids[2] + w[1] * mids[0] + neighbours(mids[1], w))

    zv = speed_of(rank // 4)
    z_rising, y_rising = rank // 4 >= HALF, rank % 4 >= 2
    shift_y = jnp.where(y_rising, 1, NY - 1)
    shift_z = jnp.where(z_rising, 1, NZ - 1)
    az = COURANT * jnp.abs(zv)

    def advance(planes, here, halves, source, beside, sink):
        u, u2, inv_t, nu, s, height = macro_state(planes)
        half_t = -0.5 * inv_t
        for i in range(NQ):
            if i // HALF in halves:
                c = xi(i) - u[0]
                c2 = c * c
                xe_ref[i] = jnp.exp(c2 * half_t)
                xc_ref[i] = c2 * inv_t
        share = 1.0 / (1.0 + nu)
        lx, lx_low = l_ref[0, here + 1], l_ref[0, here]
        lx_in = jnp.where(here < NS - 1, lx, 0.0)
        body = l_ref[3, here + 1] > 0
        out_y, in_y = sides(l_ref[1, here + 1], 0, row == 0, row == NY - 1, y_rising)
        out_z, in_z = sides(l_ref[2, here + 1], 1, lane == 0, lane == NZ - 1, z_rising)
        move = COURANT * share
        in_z = az * share * in_z
        cz = zv - u[2]
        out_x = (move * lx_low, move * lx)
        in_x = (move * lx_in, move * lx_low)

        @pl.loop(0, LY)
        def _(jy):
            yv = speed_of(rank % 4 * LY + jy)
            ay = COURANT * jnp.abs(yv)
            cy = yv - u[1]
            c2 = cy * cy + cz * cz
            top = nu * share * height * jnp.exp(c2 * half_t)
            tilt = cy * s[1] + cz * s[2] - u[0] * s[0]
            lift = c2 * inv_t - 5.0
            keep = share * (1.0 - ay * out_y - az * out_z)
            from_y = ay * share * in_y
            for i in range(NQ):
                side = i // HALF
                if side in halves:
                    f = source(jy, i)
                    a = abs(xi(i))
                    goal = top * xe_ref[i] * (1.0 + (xi(i) * s[0] + tilt) * (xc_ref[i] + lift))
                    fresh = f * (keep - a * out_x[side]) + (a * in_x[side]) * beside(jy, i)
                    fresh = fresh + from_y * pltpu.roll(f, shift_y, 0) + in_z * pltpu.roll(f, shift_z, 1)
                    sink[jy * NQ + i] = jnp.where(body, f, fresh + goal)

    def half_of(neg_ref, pos_ref):
        return lambda jy, i: (pos_ref if i >= HALF else neg_ref)[jy * HALF + i % HALF]

    def whole(ref):
        return lambda jy, i: ref[jy * NQ + i]

    before, after = jnp.maximum(slab - 1, 0), jnp.minimum(slab + 1, NS - 1)
    near, far = half_of(n1_ref, p1_ref), half_of(n2_ref, p2_ref)
    for here, halves, source, beside, sink in (
        (slab, (0, 1), whole(f_ref), near, f1_ref),
        (before, (1,), near, far, h1_ref),
        (after, (0,), near, far, h1_ref),
    ):
        advance([pred_ref[k, here] for k in range(8)], here, halves, source, beside, sink)
    advance(last, slab, (0, 1), whole(f1_ref), whole(h1_ref), out_ref)


def call(kernel, out, args, scratch=()):
    smem = pl.BlockSpec(memory_space=pltpu.SMEM)
    vmem = pl.BlockSpec(memory_space=pltpu.VMEM)
    return pl.pallas_call(
        kernel,
        out_shape=jax.ShapeDtypeStruct(out, F32),
        in_specs=[smem] + [vmem] * (len(args) - 1),
        out_specs=vmem,
        scratch_shapes=[pltpu.VMEM(s, F32) for s in scratch],
    )(*args)


def shifted(block, distance):
    count = NS
    return lax.ppermute(block, SLAB, [(i, i + distance) for i in range(count) if 0 <= i + distance < count])


def body(f_start, links, solid):
    rank, slab = lax.axis_index(VEL), lax.axis_index(SLAB)
    place = jnp.stack([rank, slab]).astype(jnp.int32)
    f = f_start.reshape(LY * NQ, NY, NZ)
    links = links.reshape(3, NY, NZ)
    solid = solid.reshape(NY, NZ)
    split = f.reshape(LY, 2, HALF, NY, NZ)
    falling = split[:, 0].reshape(LY * HALF, NY, NZ)
    rising = split[:, 1].reshape(LY * HALF, NY, NZ)
    p1, n1 = shifted(rising, 1), shifted(falling, -1)
    p2, n2 = shifted(rising, 2), shifted(falling, -2)

    parts = call(moments_kernel, (256, NZ), (place, f, links))
    parts = lax.all_to_all(parts.reshape(64, 4, NZ), VEL, 0, 0, tiled=True)
    owned = call(owner_kernel, (32, 8, NZ), (place, parts.reshape(32, 8, NZ), links, solid))
    owned = lax.all_to_all(owned, SLAB + ("zl",), 0, 0, tiled=True)
    block = call(combine_kernel, (16, 80, NZ), (place, owned.reshape(256, NZ)))
    got = lax.all_to_all(block, ("x", "y"), 0, 0, tiled=True)
    plane = (NY, NZ)
    out = call(
        finish_kernel,
        f.shape,
        (place, got.reshape(16, 10, 8, NZ), f, p1, p2, n1, n2),
        (
            (2, 8, NS) + plane,
            (4, NS + 2) + plane,
            (7, NS + 2) + plane,
            (8, NS) + plane,
            (8, NS + 4) + plane,
            (NQ,) + plane,
            (NQ,) + plane,
            f.shape,
            f.shape,
        ),
    )
    return out.reshape(f_start.shape)


def solution(mesh):
    fine = Mesh(mesh.devices.reshape(4, 2, 4, 4, 4), SLAB + VEL)
    in_specs = (P(VEL, SLAB, None, None), P(None, SLAB, None, None), P(SLAB, None, None))
    out_specs = P(VEL, SLAB, None, None)
    return jax.shard_map(body, mesh=fine, in_specs=in_specs, out_specs=out_specs, check_vma=False)
```

time: 1250 us -> 101 us (0.08)
  the two profiles are of different devices: /device:TPU:128 before, /device:TPU:1 now
where the time goes in v1:
time: 101 us
  blocking collectives  52.6 us (52%)
  waiting for transfers between devices  22.3 us (22%)
  starting transfers between devices  12.6 us (12%)
  Pallas kernels  11.4 us (11%)
    all_to_all x1, blocking collectives, body(): owned = lax.all_to_all(owned, SLAB + ('zl',), 0, 0, tiled=True)  30.6 us
    ppermute x4, waiting for transfers between devices, shifted(): lax.ppermute(block, SLAB, [(i, i + distance) for i in range(count) if 0 <...  22.3 us
    all_to_all x1, blocking collectives, body(): parts = lax.all_to_all(parts.reshape(64, 4, NZ), VEL, 0, 0, tiled=True)  22 us
    pallas_call x4, Pallas kernels, call(): pl.pallas_call(kernel, out_shape=jax.ShapeDtypeStruct(out, F32), in_specs...  11.4 us
    ppermute x4, starting transfers between devices, shifted(): lax.ppermute(block, SLAB, [(i, i + distance) for i in range(count) if 0 <...  8.87 us
    all_to_all x1, starting transfers between devices, body(): got = lax.all_to_all(block, ('x', 'y'), 0, 0, tiled=True)  3.72 us
  transfers between devices with their start and end apart: 5, of which 2 were waited for; matrix products, arithmetic and copies ran while one was open for 0% of the time, Pallas kernels for 0%

profile of v1, /device:TPU:1, one launch (start us, length us, event | category | flops | bytes accessed | tf_op | source)
XLA Modules:
  0.0 100.6 jit_solution(8430354763082270007)
XLA Ops:
  0.0 0.7 pad_add_fusion.place
  0.7 1.8 %shard_map.37 = f32[256,128]{1,0:T(8,128)} custom-call(s32[2]{0:T(128)} %pad_add_fusion.place, f32[64,8,128]{2,1,0:T(8,128)} %bitcast.20, s32[3,8,128]{2,1,0:T(8,128)} %bitcast.30), custom_call_target="tpu_custom_call" | custom-call | tf_op jit(solution)/shard_map/pallas_call | solution.py:373
  2.4 22.0 %all_to_all.15 = f32[64,4,128]{2,1,0:T(4,128)} all-to-all(f32[64,4,128]{2,1,0:T(4,128)} %bitcast.24), channel_id=1, replica_groups=mesh['zh'=4,'core'=2,'x'=4,'y'=4,'zl'=4] {'x','y','zl'}, dimensions={0} | all-to-all | bytes 262144 | tf_op jit(solution)/shard_map/all_to_all | solution.py:400
  24.4 1.6 %shard_map.38 = f32[32,8,128]{2,1,0:T(8,128)} custom-call(s32[2]{0:T(128)} %pad_add_fusion.place, f32[32,8,128]{2,1,0:T(8,128)} %bitcast.23, s32[3,8,128]{2,1,0:T(8,128)} %bitcast.31, s32[8,128]{1,0:T(8,128)} %bitcast.32), custom_call_target="tpu_custom_call" | custom-call | tf_op jit(solution)/shard_map/pallas_call | solution.py:373
  26.0 30.6 %all_to_all.16 = f32[32,8,128]{2,1,0:T(8,128)} all-to-all(f32[32,8,128]{2,1,0:T(8,128)} %shard_map.38), channel_id=1, replica_groups=mesh['zh'=4,'core'=2,'x'=4,'y'=4,'zl'=4] {'zh','core','zl'}, dimensions={0} | all-to-all | bytes 262144 | tf_op jit(solution)/shard_map/all_to_all | solution.py:402
  56.7 1.8 %shard_map.39 = f32[16,80,128]{2,1,0:T(8,128)} custom-call(s32[2]{0:T(128)} %pad_add_fusion.place, f32[256,128]{1,0:T(8,128)} %bitcast.25), custom_call_target="tpu_custom_call" | custom-call | tf_op jit(solution)/shard_map/pallas_call | solution.py:373
  58.5 0.0 copy-start.1
  58.5 3.7 %all-to-all-start.2 = ((f32[16,80,128]{2,1,0:T(8,128)}), f32[16,80,128]{2,1,0:T(8,128)S(1)}, u32[]{:S(2)}, u32[]{:S(2)}) async-start(f32[16,80,128]{2,1,0:T(8,128)} %shard_map.39), calls=%async_computation.2 | async-start | bytes 1310720 | tf_op jit(solution)/shard_map/all_to_all | solution.py:404
  62.2 0.0 copy-done.1
  62.2 3.3 %collective-permute-start = (f32[32,8,128]{2,1,0:T(8,128)S(1)}, f32[32,8,128]{2,1,0:T(8,128)S(1)}, u32[]{:S(2)}, u32[]{:S(2)}) collective-permute-start(f32[32,8,128]{2,1,0:T(8,128)S(1)} %bitcast.28), channel_id=1, source_target_pairs={{0,64},{64,128},{128,192},{192,256},{256,320},{320,384},{384,448},... | collective-permute-start | bytes 393224 | tf_op jit(solution)/shard_map/ppermute | solution.py:384
  65.5 2.3 %collective-permute-start.1 = (f32[32,8,128]{2,1,0:T(8,128)S(1)}, f32[32,8,128]{2,1,0:T(8,128)S(1)}, u32[]{:S(2)}, u32[]{:S(2)}) collective-permute-start(f32[32,8,128]{2,1,0:T(8,128)S(1)} %bitcast.29), channel_id=1, source_target_pairs={{0,128},{64,192},{128,256},{192,320},{256,384},{320,448},{1,129},{... | collective-permute-start | bytes 393224 | tf_op jit(solution)/shard_map/ppermute | solution.py:384
  67.8 2.1 %collective-permute-start.2 = (f32[32,8,128]{2,1,0:T(8,128)S(1)}, f32[32,8,128]{2,1,0:T(8,128)S(1)}, u32[]{:S(2)}, u32[]{:S(2)}) collective-permute-start(f32[32,8,128]{2,1,0:T(8,128)S(1)} %bitcast.26), channel_id=1, source_target_pairs={{64,0},{128,64},{192,128},{256,192},{320,256},{384,320},{448,384},... | collective-permute-start | bytes 393224 | tf_op jit(solution)/shard_map/ppermute | solution.py:384
  69.8 1.3 %collective-permute-start.3 = (f32[32,8,128]{2,1,0:T(8,128)S(1)}, f32[32,8,128]{2,1,0:T(8,128)S(1)}, u32[]{:S(2)}, u32[]{:S(2)}) collective-permute-start(f32[32,8,128]{2,1,0:T(8,128)S(1)} %bitcast.27), channel_id=1, source_target_pairs={{128,0},{192,64},{256,128},{320,192},{384,256},{448,320},{129,1},{... | collective-permute-start | bytes 393224 | tf_op jit(solution)/shard_map/ppermute | solution.py:384
  71.1 0.0 collective-permute-done.p1_ref
  71.1 0.0 copy-start.2
  71.2 0.0 collective-permute-done.1.p2_ref
  71.2 0.0 copy-start.3
  71.2 19.7 %collective-permute-done.2.n1_ref = f32[32,8,128]{2,1,0:T(8,128)S(1)} collective-permute-done((f32[32,8,128]{2,1,0:T(8,128)S(1)}, f32[32,8,128]{2,1,0:T(8,128)S(1)}, u32[]{:S(2)}, u32[]{:S(2)}) %collective-permute-start.2) | collective-permute-done | bytes 131104 | tf_op jit(solution)/shard_map/ppermute | solution.py:384
  90.8 0.0 copy-start.4
  90.8 2.6 %collective-permute-done.3.n2_ref = f32[32,8,128]{2,1,0:T(8,128)S(1)} collective-permute-done((f32[32,8,128]{2,1,0:T(8,128)S(1)}, f32[32,8,128]{2,1,0:T(8,128)S(1)}, u32[]{:S(2)}, u32[]{:S(2)}) %collective-permute-start.3) | collective-permute-done | bytes 131104 | tf_op jit(solution)/shard_map/ppermute | solution.py:384
  93.4 0.0 copy-start.5
  93.4 0.0 all-to-all-done.2
  93.5 0.0 copy-start
  93.5 0.0 copy-done.2
  93.5 0.0 copy-done.3
  93.5 0.0 copy-done.4
  93.5 0.6 copy-done.5
  94.1 0.2 copy-done
  94.3 6.2 %shard_map.40 = f32[64,8,128]{2,1,0:T(8,128)} custom-call(s32[2]{0:T(128)} %pad_add_fusion.place, f32[16,10,8,128]{3,2,1,0:T(8,128)} %bitcast.19, f32[64,8,128]{2,1,0:T(8,128)} %bitcast.21, f32[32,8,128]{2,1,0:T(8,128)} %copy-done.2, f32[32,8,128]{2,1,0:T(8,128)} %copy-done.3, f32[32,8,128]{2,1,0:T(8,128)} %copy-done.4, f32[32,8,128]{2,1,0:T(8,128)} %copy-done.5), custom_call_target="tpu_custom_call" | custom-call | tf_op jit(solution)/shard_map/pallas_call | solution.py:373
  (1 shorter events, 0.0 us)
Async XLA Ops:
  58.5 3.7 %copy-start.1 = (f32[64,1,8,128]{3,2,1,0:T(8,128)S(1)}, f32[64,1,8,128]{3,2,1,0:T(8,128)}, u32[]{:S(2)}) copy-start(f32[64,1,8,128]{3,2,1,0:T(8,128)} %param.3) | copy-start | bytes 786436
  58.5 35.0 %all-to-all-start.2 = ((f32[16,80,128]{2,1,0:T(8,128)}), f32[16,80,128]{2,1,0:T(8,128)S(1)}, u32[]{:S(2)}, u32[]{:S(2)}) async-start(f32[16,80,128]{2,1,0:T(8,128)} %shard_map.39), calls=%async_computation.2 | async-start | bytes 1310720 | tf_op jit(solution)/shard_map/all_to_all | solution.py:404
  62.2 8.9 %collective-permute-start = (f32[32,8,128]{2,1,0:T(8,128)S(1)}, f32[32,8,128]{2,1,0:T(8,128)S(1)}, u32[]{:S(2)}, u32[]{:S(2)}) collective-permute-start(f32[32,8,128]{2,1,0:T(8,128)S(1)} %bitcast.28), channel_id=1, source_target_pairs={{0,64},{64,128},{128,192},{192,256},{256,320},{320,384},{384,448},... | collective-permute-start | bytes 393224 | tf_op jit(solution)/shard_map/ppermute | solution.py:384
  65.5 5.7 %collective-permute-start.1 = (f32[32,8,128]{2,1,0:T(8,128)S(1)}, f32[32,8,128]{2,1,0:T(8,128)S(1)}, u32[]{:S(2)}, u32[]{:S(2)}) collective-permute-start(f32[32,8,128]{2,1,0:T(8,128)S(1)} %bitcast.29), channel_id=1, source_target_pairs={{0,128},{64,192},{128,256},{192,320},{256,384},{320,448},{1,129},{... | collective-permute-start | bytes 393224 | tf_op jit(solution)/shard_map/ppermute | solution.py:384
  67.8 23.1 %collective-permute-start.2 = (f32[32,8,128]{2,1,0:T(8,128)S(1)}, f32[32,8,128]{2,1,0:T(8,128)S(1)}, u32[]{:S(2)}, u32[]{:S(2)}) collective-permute-start(f32[32,8,128]{2,1,0:T(8,128)S(1)} %bitcast.26), channel_id=1, source_target_pairs={{64,0},{128,64},{192,128},{256,192},{320,256},{384,320},{448,384},... | collective-permute-start | bytes 393224 | tf_op jit(solution)/shard_map/ppermute | solution.py:384
  69.8 23.6 %collective-permute-start.3 = (f32[32,8,128]{2,1,0:T(8,128)S(1)}, f32[32,8,128]{2,1,0:T(8,128)S(1)}, u32[]{:S(2)}, u32[]{:S(2)}) collective-permute-start(f32[32,8,128]{2,1,0:T(8,128)S(1)} %bitcast.27), channel_id=1, source_target_pairs={{128,0},{192,64},{256,128},{320,192},{384,256},{448,320},{129,1},{... | collective-permute-start | bytes 393224 | tf_op jit(solution)/shard_map/ppermute | solution.py:384
  71.1 22.3 %copy-start.2 = (f32[32,8,128]{2,1,0:T(8,128)}, f32[32,8,128]{2,1,0:T(8,128)S(1)}, u32[]{:S(2)}) copy-start(f32[32,8,128]{2,1,0:T(8,128)S(1)} %collective-permute-done.p1_ref) | copy-start | bytes 393220
  71.2 22.3 %copy-start.3 = (f32[32,8,128]{2,1,0:T(8,128)}, f32[32,8,128]{2,1,0:T(8,128)S(1)}, u32[]{:S(2)}) copy-start(f32[32,8,128]{2,1,0:T(8,128)S(1)} %collective-permute-done.1.p2_ref) | copy-start | bytes 393220
  90.8 2.6 %copy-start.4 = (f32[32,8,128]{2,1,0:T(8,128)}, f32[32,8,128]{2,1,0:T(8,128)S(1)}, u32[]{:S(2)}) copy-start(f32[32,8,128]{2,1,0:T(8,128)S(1)} %collective-permute-done.2.n1_ref) | copy-start | bytes 393220
  93.4 0.6 copy-start.5
  93.5 0.9 copy-start

commit v2 on v1

--- a/solution.py
+++ b/solution.py
@@ -7,6 +7,7 @@
 from jax.experimental.pallas import tpu as pltpu
 from jax.sharding import Mesh
 from jax.sharding import PartitionSpec as P
+
 
 NQ = 16
 HALF = NQ // 2
@@ -19,6 +20,7 @@
 VISCOUS_TO_HEAT = 2.0 / 3.0
 QUAD_WEIGHT = SPACING**3 / (2.0 * math.pi) ** 1.5
 F32 = jnp.float32
+LIMIT = 4 << 20
 
 SLAB = ("zh", "core")
 VEL = ("x", "y", "zl")
@@ -49,8 +51,12 @@
     return jnp.where(rising, open_up, open_low), jnp.where(rising, open_low, inner_up)
 
 
-def moments_kernel(place, f_ref, links_ref, out_ref):
-    rank = place[0]
+def moments_kernel(f_ref, links_ref, out_ref, inner_ref, outer_ref):
+    core = lax.axis_index("core")
+    for jy in range(LY):
+        inner_ref[pl.ds(jy * HALF, HALF)] = f_ref[pl.ds(jy * NQ + (1 - core) * HALF, HALF)]
+        outer_ref[pl.ds(jy * HALF, HALF)] = f_ref[pl.ds(jy * NQ + core * HALF, HALF)]
+    rank = lax.axis_index(VEL)
     row, lane = rows_and_lanes()
     zv = speed_of(rank // 4)
     z_rising, y_rising = rank // 4 >= HALF, rank % 4 >= 2
@@ -99,8 +105,8 @@
             out_ref[pl.ds(k * 32 + kind, NY, stride=4), :] = v * QUAD_WEIGHT
 
 
-def owner_kernel(place, parts_ref, links_ref, solid_ref, out_ref):
-    rank = place[0]
+def owner_kernel(parts_ref, links_ref, solid_ref, out_ref):
+    rank = lax.axis_index(VEL)
     k, y = rank // 8, rank % 8
     total = parts_ref[0]
     for i in range(1, 32):
@@ -112,23 +118,24 @@
     kind = k % 4
     own = jnp.where(kind == 0, flags[0], jnp.where(kind == 1, flags[1], jnp.where(kind == 2, flags[2], flags[3])))
     block = jnp.where(row < 4, total, jnp.where(row == 4, flags[0], jnp.where(row == 5, own, 0.0)))
-    for i in range(out_ref.shape[0]):
-        out_ref[i] = block
-
-
-def combine_kernel(place, parts_ref, out_ref):
-    rank = place[0]
-    kinds = [parts_ref[pl.ds(kind, 32, stride=8), :] for kind in range(6)]
+    for i in range(32):
+        out_ref[pl.ds(6 * i, 6), :] = block[:6]
+
+
+def combine_kernel(parts_ref, out_ref):
+    rank = lax.axis_index(VEL)
+    kinds = [parts_ref[pl.ds(kind, 32, stride=6), :] for kind in range(6)]
     m0, q, hp, hm, lx, own = kinds
     row = lax.broadcasted_iota(jnp.int32, (32, NZ), 0)
     low = jnp.where(row < 4, 0.0, pltpu.roll(lx, 4, 0))
     inner = jnp.where(row >= 28, 0.0, lx)
     mt = q - COURANT * (lx * hp + low * hm - low * pltpu.roll(hp, 4, 0) - inner * pltpu.roll(hm, 28, 0))
     half = jnp.where(rank // 32 == 0, own[:16], own[16:])
+    mt_near = jnp.where(lax.axis_index(SLAB) < NS // 2, mt[:24], mt[8:])
     for i in range(out_ref.shape[0]):
         out_ref[i, 0:32, :] = m0
-        out_ref[i, 32:64, :] = mt
-        out_ref[i, 64:80, :] = half
+        out_ref[i, 32:56, :] = mt_near
+        out_ref[i, 56:72, :] = half
 
 
 def macro_state(p):
@@ -165,42 +172,46 @@
                     t = t * c
         one_d.append(m)
     x, y, z = one_d
-    s5 = [-5.0 * v for v in s]
-    st = [v * inv_t for v in s]
-    cache = {}
+    made = {}
+
+    def once(key, build):
+        if key not in made:
+            made[key] = build()
+        return made[key]
 
     def xy(i, j):
-        if (i, j) not in cache:
-            cache[i, j] = x[i] * y[j]
-        return cache[i, j]
+        return once(("xy", i, j), lambda: x[i] * y[j])
+
+    def xy2(i, j):
+        return once(("xy2", i, j), lambda: xy(i + 2, j) + xy(i, j + 2))
 
     def plain(i, j, k):
-        return xy(i, j) * z[k]
-
-    def mean(i, j, k):
-        total = plain(i, j, k)
-        for a in range(3):
-            e = [i, j, k]
-            e[a] += 1
-            square = None
-            for b in range(3):
-                d = list(e)
-                d[b] += 2
-                t = plain(*d)
-                square = t if square is None else square + t
-            total = total + s5[a] * plain(*e) + st[a] * square
-        return total
+        return once(("plain", i, j, k), lambda: xy(i, j) * z[k])
+
+    def squared(i, j, k):
+        return once(("squared", i, j, k), lambda: xy2(i, j) * z[k] + xy(i, j) * z[k + 2])
+
+    def tilted(i, j, k):
+        return once(("tilted", i, j, k), lambda: squared(i, j, k) * inv_t - 5.0 * plain(i, j, k))
+
+    def tilted2(i, j, k):
+        def build():
+            xy4 = once(("xy4", i, j), lambda: xy2(i + 2, j) + xy2(i, j + 2))
+            fourth = xy4 * z[k] + 2.0 * (xy2(i, j) * z[k + 2]) + xy(i, j) * z[k + 4]
+            return fourth * inv_t - 5.0 * squared(i, j, k)
+
+        return once(("tilted2", i, j, k), build)
 
     def unit(*axes):
-        e = [0, 0, 0]
-        for a in axes:
-            e[a] += 1
-        return mean(*e)
-
-    n0 = unit()
-    n1 = [unit(a) for a in range(3)]
-    n2 = {(a, b): unit(a, b) for a in range(3) for b in range(a, 3)}
-    n3 = [unit(a, 0, 0) + unit(a, 1, 1) + unit(a, 2, 2) for a in range(3)]
+        return tuple(axes.count(a) for a in range(3))
+
+    def mean(first, with_c, *axes):
+        return first(*unit(*axes)) + sum(s[a] * with_c(*unit(*axes, a)) for a in range(3))
+
+    n0 = mean(plain, tilted)
+    n1 = [mean(plain, tilted, a) for a in range(3)]
+    n2 = {(a, b): mean(plain, tilted, a, b) for a in range(3) for b in range(a, 3)}
+    n3 = [mean(squared, tilted2, a) for a in range(3)]
     weight = QUAD_WEIGHT * height
     j_e = 0.5 * (n2[0, 0] + n2[1, 1] + n2[2, 2] + u2 * n0) + u[0] * n1[0] + u[1] * n1[1] + u[2] * n1[2]
     rows = [n0] + [n1[a] + u[a] * n0 for a in range(3)] + [j_e]
@@ -215,10 +226,10 @@
 
 
 def finish_kernel(
-    place, got_ref, f_ref, p1_ref, p2_ref, n1_ref, n2_ref, out_ref, m_ref, l_ref, w_ref, pred_ref, next_ref,
+    got_ref, f_ref, inner1_ref, inner2_ref, outer1_ref, outer2_ref, out_ref, m_ref, l_ref, w_ref, pred_ref, next_ref,
     xe_ref, xc_ref, f1_ref, h1_ref,
 ):
-    rank, slab = place[0], place[1]
+    rank, slab, core = lax.axis_index(VEL), lax.axis_index(SLAB), lax.axis_index("core")
     row, lane = rows_and_lanes()
     low_half = row < 4
     zero = jnp.zeros((NY, NZ), F32)
@@ -229,15 +240,15 @@
 
     @pl.loop(0, 8)
     def _(k):
-        for t in range(10):
+        for t in range(9):
             t0, t1 = got_ref[2 * k, t], got_ref[2 * k + 1, t]
             first = jnp.where(low_half, t0, pltpu.roll(t1, 4, 0))
             second = jnp.where(low_half, pltpu.roll(t0, 4, 0), t1)
-            if t < 8:
+            if t < 7:
                 m_ref[t // 4, k, 2 * (t % 4)] = first
                 m_ref[t // 4, k, 2 * (t % 4) + 1] = second
             else:
-                base = 1 + k // 4 * 4 + 2 * (t - 8)
+                base = 1 + k // 4 * 4 + 2 * (t - 7)
                 l_ref[k % 4, base] = first
                 l_ref[k % 4, base + 1] = second
 
@@ -280,6 +291,8 @@
         for i in (0, 1, NS + 2, NS + 3):
             next_ref[k, i] = zero
 
+    shift = jnp.where(slab < NS // 2, 0, 2)
+
     @pl.loop(jnp.maximum(slab - 2, 0), jnp.minimum(slab + 3, NS))
     def _(w):
         u, u2, inv_t, nu, s, height = macro_state([pred_ref[k, w] for k in range(8)])
@@ -287,7 +300,7 @@
         body = l_ref[3, w + 1] > 0
         share = 1.0 / (1.0 + nu)
         for k in range(8):
-            fresh = (m_ref[1, k, w] + nu * goal[k]) * share
+            fresh = (m_ref[1, k, w - shift] + nu * goal[k]) * share
             next_ref[k, w + 2] = jnp.where(body, m_ref[0, k, w], fresh)
 
     last = []
@@ -309,7 +322,7 @@
     az = COURANT * jnp.abs(zv)
 
     def advance(planes, here, halves, source, beside, sink):
-        u, u2, inv_t, nu, s, height = macro_state(planes)
+        u, _, inv_t, nu, s, height = macro_state(planes)
         half_t = -0.5 * inv_t
         for i in range(NQ):
             if i // HALF in halves:
@@ -350,14 +363,19 @@
                     fresh = fresh + from_y * pltpu.roll(f, shift_y, 0) + in_z * pltpu.roll(f, shift_z, 1)
                     sink[jy * NQ + i] = jnp.where(body, f, fresh + goal)
 
-    def half_of(neg_ref, pos_ref):
-        return lambda jy, i: (pos_ref if i >= HALF else neg_ref)[jy * HALF + i % HALF]
+    def halo(inner_ref, outer_ref):
+        def load(jy, i):
+            j = jy * HALF + i % HALF
+            on_chip = core == (0 if i < HALF else 1)
+            return jnp.where(on_chip, inner_ref[j], outer_ref[j])
+
+        return load
 
     def whole(ref):
         return lambda jy, i: ref[jy * NQ + i]
 
     before, after = jnp.maximum(slab - 1, 0), jnp.minimum(slab + 1, NS - 1)
-    near, far = half_of(n1_ref, p1_ref), half_of(n2_ref, p2_ref)
+    near, far = halo(inner1_ref, outer1_ref), halo(inner2_ref, outer2_ref)
     for here, halves, source, beside, sink in (
         (slab, (0, 1), whole(f_ref), near, f1_ref),
         (before, (1,), near, far, h1_ref),
@@ -367,46 +385,47 @@
     advance(last, slab, (0, 1), whole(f1_ref), whole(h1_ref), out_ref)
 
 
-def call(kernel, out, args, scratch=()):
-    smem = pl.BlockSpec(memory_space=pltpu.SMEM)
+def call(kernel, out, args, scratch=(), limit=None, keep=pltpu.VMEM):
     vmem = pl.BlockSpec(memory_space=pltpu.VMEM)
     return pl.pallas_call(
         kernel,
-        out_shape=jax.ShapeDtypeStruct(out, F32),
-        in_specs=[smem] + [vmem] * (len(args) - 1),
-        out_specs=vmem,
+        out_shape=[keep(shape, F32) for shape in out],
+        in_specs=[vmem] * len(args),
+        out_specs=[vmem] * len(out),
         scratch_shapes=[pltpu.VMEM(s, F32) for s in scratch],
+        compiler_params=pltpu.CompilerParams(vmem_limit_bytes=limit),
     )(*args)
 
 
-def shifted(block, distance):
-    count = NS
-    return lax.ppermute(block, SLAB, [(i, i + distance) for i in range(count) if 0 <= i + distance < count])
-
-
-def body(f_start, links, solid):
-    rank, slab = lax.axis_index(VEL), lax.axis_index(SLAB)
-    place = jnp.stack([rank, slab]).astype(jnp.int32)
+def over_chip(block):
+    return lax.ppermute(block, "core", [(0, 1), (1, 0)])
+
+
+def to_next_chip(block):
+    pairs = [(i, i + 1) for i in range(1, NS - 1, 2)]
+    return lax.ppermute(block, SLAB, pairs + [(b, a) for a, b in pairs])
+
+
+def steps(f_start, links, solid):
     f = f_start.reshape(LY * NQ, NY, NZ)
     links = links.reshape(3, NY, NZ)
     solid = solid.reshape(NY, NZ)
-    split = f.reshape(LY, 2, HALF, NY, NZ)
-    falling = split[:, 0].reshape(LY * HALF, NY, NZ)
-    rising = split[:, 1].reshape(LY * HALF, NY, NZ)
-    p1, n1 = shifted(rising, 1), shifted(falling, -1)
-    p2, n2 = shifted(rising, 2), shifted(falling, -2)
-
-    parts = call(moments_kernel, (256, NZ), (place, f, links))
+    half = (LY * HALF, NY, NZ)
+    parts, to_inner, to_outer = call(moments_kernel, ((256, NZ), half, half), (f, links))
+    outer1 = to_next_chip(to_outer)
+    inner1 = over_chip(to_inner)
     parts = lax.all_to_all(parts.reshape(64, 4, NZ), VEL, 0, 0, tiled=True)
-    owned = call(owner_kernel, (32, 8, NZ), (place, parts.reshape(32, 8, NZ), links, solid))
-    owned = lax.all_to_all(owned, SLAB + ("zl",), 0, 0, tiled=True)
-    block = call(combine_kernel, (16, 80, NZ), (place, owned.reshape(256, NZ)))
+    (owned,) = call(owner_kernel, ((192, NZ),), (parts.reshape(32, 8, NZ), links, solid), limit=LIMIT)
+    owned = lax.all_to_all(owned.reshape(32, 1, 6 * NZ), SLAB + ("zl",), 0, 0, tiled=True)
+    outer2 = to_next_chip(inner1)
+    inner2 = over_chip(outer1)
+    (block,) = call(combine_kernel, ((16, 72, NZ),), (owned.reshape(192, NZ),), limit=LIMIT)
     got = lax.all_to_all(block, ("x", "y"), 0, 0, tiled=True)
     plane = (NY, NZ)
-    out = call(
+    (out,) = call(
         finish_kernel,
-        f.shape,
-        (place, got.reshape(16, 10, 8, NZ), f, p1, p2, n1, n2),
+        (f.shape,),
+        (got.reshape(16, 9, 8, NZ), f, inner1, inner2, outer1, outer2),
         (
             (2, 8, NS) + plane,
             (4, NS + 2) + plane,
@@ -418,6 +437,8 @@
             f.shape,
             f.shape,
         ),
+        limit=16 << 20,
+        keep=jax.ShapeDtypeStruct,
     )
     return out.reshape(f_start.shape)
 
@@ -426,4 +447,4 @@
     fine = Mesh(mesh.devices.reshape(4, 2, 4, 4, 4), SLAB + VEL)
     in_specs = (P(VEL, SLAB, None, None), P(None, SLAB, None, None), P(SLAB, None, None))
     out_specs = P(VEL, SLAB, None, None)
-    return jax.shard_map(body, mesh=fine, in_specs=in_specs, out_specs=out_specs, check_vma=False)
+    return jax.shard_map(steps, mesh=fine, in_specs=in_specs, out_specs=out_specs, check_vma=False)

time: 101 us -> 89.8 us (0.89)
  waiting for transfers between devices: 22.3 us -> 17.5 us
  Pallas kernels: 11.4 us -> 6.87 us
  blocking collectives: 52.6 us -> 50.6 us
  starting transfers between devices: 12.6 us -> 14.4 us
    ppermute x4, waiting for transfers between devices: 22.3 us -> 17.5 us  [the longest x2 17.4 us: to_next_chip(): return lax.ppermute(block, SLAB, pairs + [(b, a) for a, b in pairs])]
    pallas_call x4, Pallas kernels: 11.4 us -> 6.87 us  [call(): pl.pallas_call(kernel, out_shape=[keep(shape, F32) for shape in out], in_...]
    all_to_all x2, blocking collectives: 52.6 us -> 50.6 us  [the longest x1 28.9 us: steps(): lax.all_to_all(owned.reshape(32, 1, 6 * NZ), SLAB + ('zl',), 0, 0, tiled=...]
    ppermute x4, starting transfers between devices: 8.87 us -> 10.6 us  [the longest x2 6.82 us: to_next_chip(): return lax.ppermute(block, SLAB, pairs + [(b, a) for a, b in pairs])]
where the time goes in v2:
time: 89.8 us; the launch traced here: 89.4 us
  blocking collectives  50.6 us (56%)
  waiting for transfers between devices  17.5 us (19%)
  starting transfers between devices  14.4 us (16%)
  Pallas kernels  6.87 us (8%)
    all_to_all x1, blocking collectives, steps(): lax.all_to_all(owned.reshape(32, 1, 6 * NZ), SLAB + ('zl',), 0, 0, tiled=...  28.9 us
    all_to_all x1, blocking collectives, steps(): parts = lax.all_to_all(parts.reshape(64, 4, NZ), VEL, 0, 0, tiled=True)  21.7 us
    ppermute x2, waiting for transfers between devices, to_next_chip(): return lax.ppermute(block, SLAB, pairs + [(b, a) for a, b in pairs])  17.4 us
    pallas_call x4, Pallas kernels, call(): pl.pallas_call(kernel, out_shape=[keep(shape, F32) for shape in out], in_...  6.87 us
    ppermute x2, starting transfers between devices, to_next_chip(): return lax.ppermute(block, SLAB, pairs + [(b, a) for a, b in pairs])  6.82 us
    ppermute x2, starting transfers between devices, over_chip(): return lax.ppermute(block, 'core', [(0, 1), (1, 0)])  3.83 us
    all_to_all x1, starting transfers between devices, steps(): got = lax.all_to_all(block, ('x', 'y'), 0, 0, tiled=True)  3.71 us
  transfers between devices with their start and end apart: 5, of which 2 were waited for; matrix products, arithmetic and copies ran while one was open for 0% of the time, Pallas kernels for 0%

profile of v2, /device:TPU:1, one launch (start us, length us, event | category | flops | bytes accessed | tf_op | source)
XLA Modules:
  0.0 89.4 jit_solution(8912806547397308184)
XLA Ops:
  0.0 1.1 %shard_map.37 = (f32[256,128]{1,0:T(8,128)S(1)}, f32[32,8,128]{2,1,0:T(8,128)S(1)}, f32[32,8,128]{2,1,0:T(8,128)S(1)}) custom-call(f32[64,8,128]{2,1,0:T(8,128)} %bitcast.12, s32[3,8,128]{2,1,0:T(8,128)} %bitcast.18), custom_call_target="tpu_custom_call" | custom-call | tf_op jit(solution)/shard_map/pallas_call | solution.py:390
  1.1 0.0 copy-start.1
  1.1 0.0 copy-start.2
  1.1 21.7 %all_to_all.15 = f32[64,4,128]{2,1,0:T(4,128)S(1)} all-to-all(f32[64,4,128]{2,1,0:T(4,128)S(1)} %bitcast.17), channel_id=1, replica_groups=mesh['zh'=4,'core'=2,'x'=4,'y'=4,'zl'=4] {'x','y','zl'}, dimensions={0} | all-to-all | bytes 262144 | tf_op jit(solution)/shard_map/all_to_all | solution.py:417
  22.8 0.0 copy-done.1
  22.8 0.0 copy-done.2
  22.9 28.9 %all_to_all.16 = f32[32,1,768]{2,1,0:T(1,128)S(1)} all-to-all(f32[32,1,768]{2,1,0:T(1,128)S(1)} %bitcast.15), channel_id=1, replica_groups=mesh['zh'=4,'core'=2,'x'=4,'y'=4,'zl'=4] {'zh','core','zl'}, dimensions={0} | all-to-all | bytes 196608 | tf_op jit(solution)/shard_map/all_to_all | solution.py:419
  51.8 0.9 shard_map.39
  52.7 0.0 copy-start
  52.7 3.7 %all-to-all-start.2 = ((f32[16,72,128]{2,1,0:T(8,128)}), f32[16,72,128]{2,1,0:T(8,128)S(1)}, u32[]{:S(2)}, u32[]{:S(2)}) async-start(f32[16,72,128]{2,1,0:T(8,128)} %shard_map.39), calls=%async_computation.2 | async-start | bytes 1179648 | tf_op jit(solution)/shard_map/all_to_all | solution.py:423
  56.4 3.3 %collective-permute-start.1 = (f32[32,8,128]{2,1,0:T(8,128)S(1)}, f32[32,8,128]{2,1,0:T(8,128)S(1)}, u32[]{:S(2)}, u32[]{:S(2)}) collective-permute-start(f32[32,8,128]{2,1,0:T(8,128)S(1)} %get-tuple-element.10), channel_id=1, source_target_pairs={{64,128},{192,256},{320,384},{128,64},{256,192},{384,320},{65,129}... | collective-permute-start | bytes 393224 | tf_op jit(solution)/shard_map/ppermute | solution.py:406
  59.7 1.9 %collective-permute-start = (f32[32,8,128]{2,1,0:T(8,128)S(1)}, f32[32,8,128]{2,1,0:T(8,128)S(1)}, u32[]{:S(2)}, u32[]{:S(2)}) collective-permute-start(f32[32,8,128]{2,1,0:T(8,128)S(1)} %get-tuple-element.9), channel_id=1, source_target_pairs={{0,64},{64,0},{1,65},{65,1},{2,66},{66,2},{3,67},{67,3},{4,68},{68... | collective-permute-start | bytes 393224 | tf_op jit(solution)/shard_map/ppermute | solution.py:401
  61.6 8.9 %collective-permute-done.1.outer1_ref = f32[32,8,128]{2,1,0:T(8,128)S(1)} collective-permute-done((f32[32,8,128]{2,1,0:T(8,128)S(1)}, f32[32,8,128]{2,1,0:T(8,128)S(1)}, u32[]{:S(2)}, u32[]{:S(2)}) %collective-permute-start.1) | collective-permute-done | bytes 131104 | tf_op jit(solution)/shard_map/ppermute | solution.py:406
  70.6 1.9 %collective-permute-start.2 = (f32[32,8,128]{2,1,0:T(8,128)S(1)}, f32[32,8,128]{2,1,0:T(8,128)S(1)}, u32[]{:S(2)}, u32[]{:S(2)}) collective-permute-start(f32[32,8,128]{2,1,0:T(8,128)S(1)} %collective-permute-done.1.outer1_ref), channel_id=1, source_target_pairs={{0,64},{64,0},{1,65},{65,1},{2,66},{66,2},{3,67},{67,3},{4,68},{68... | collective-permute-start | bytes 393224 | tf_op jit(solution)/shard_map/ppermute | solution.py:401
  72.5 0.0 collective-permute-done.inner1_ref
  72.5 3.5 %collective-permute-start.3 = (f32[32,8,128]{2,1,0:T(8,128)S(1)}, f32[32,8,128]{2,1,0:T(8,128)S(1)}, u32[]{:S(2)}, u32[]{:S(2)}) collective-permute-start(f32[32,8,128]{2,1,0:T(8,128)S(1)} %collective-permute-done.inner1_ref), channel_id=1, source_target_pairs={{64,128},{192,256},{320,384},{128,64},{256,192},{384,320},{65,129}... | collective-permute-start | bytes 393224 | tf_op jit(solution)/shard_map/ppermute | solution.py:406
  76.0 0.0 collective-permute-done.2.inner2_ref
  76.0 8.5 %collective-permute-done.3.outer2_ref = f32[32,8,128]{2,1,0:T(8,128)S(1)} collective-permute-done((f32[32,8,128]{2,1,0:T(8,128)S(1)}, f32[32,8,128]{2,1,0:T(8,128)S(1)}, u32[]{:S(2)}, u32[]{:S(2)}) %collective-permute-start.3) | collective-permute-done | bytes 131104 | tf_op jit(solution)/shard_map/ppermute | solution.py:406
  84.5 0.0 all-to-all-done.2
  84.5 0.0 copy-done
  84.5 4.8 %shard_map.40 = f32[64,8,128]{2,1,0:T(8,128)} custom-call(f32[16,9,8,128]{3,2,1,0:T(8,128)S(1)} %bitcast.11, f32[64,8,128]{2,1,0:T(8,128)S(1)} %bitcast.13, f32[32,8,128]{2,1,0:T(8,128)S(1)} %collective-permute-done.inner1_ref, f32[32,8,128]{2,1,0:T(8,128)S(1)} %collective-permute-done.2.inner2_ref, f32[32,8,128]{2,1,0:T(8,128)S(1)} %collective-permute-done.1.outer1_ref, ...), custom_call_target="tpu_custom_call" | custom-call | tf_op jit(solution)/shard_map/pallas_call | solution.py:390
  (1 shorter events, 0.0 us)
Async XLA Ops:
  1.1 21.7 %copy-start.1 = (s32[3,1,8,128]{3,2,1,0:T(8,128)S(1)}, s32[3,1,8,128]{3,2,1,0:T(8,128)}, u32[]{:S(2)}) copy-start(s32[3,1,8,128]{3,2,1,0:T(8,128)} %param.4) | copy-start | bytes 36868
  1.1 21.7 %copy-start.2 = (s32[1,8,128]{2,1,0:T(8,128)S(1)}, s32[1,8,128]{2,1,0:T(8,128)}, u32[]{:S(2)}) copy-start(s32[1,8,128]{2,1,0:T(8,128)} %param.5) | copy-start | bytes 12292
  52.7 31.9 %copy-start = (f32[64,1,8,128]{3,2,1,0:T(8,128)S(1)}, f32[64,1,8,128]{3,2,1,0:T(8,128)}, u32[]{:S(2)}) copy-start(f32[64,1,8,128]{3,2,1,0:T(8,128)} %param.3) | copy-start | bytes 786436
  52.7 31.9 %all-to-all-start.2 = ((f32[16,72,128]{2,1,0:T(8,128)}), f32[16,72,128]{2,1,0:T(8,128)S(1)}, u32[]{:S(2)}, u32[]{:S(2)}) async-start(f32[16,72,128]{2,1,0:T(8,128)} %shard_map.39), calls=%async_computation.2 | async-start | bytes 1179648 | tf_op jit(solution)/shard_map/all_to_all | solution.py:423
  56.4 14.2 %collective-permute-start.1 = (f32[32,8,128]{2,1,0:T(8,128)S(1)}, f32[32,8,128]{2,1,0:T(8,128)S(1)}, u32[]{:S(2)}, u32[]{:S(2)}) collective-permute-start(f32[32,8,128]{2,1,0:T(8,128)S(1)} %get-tuple-element.10), channel_id=1, source_target_pairs={{64,128},{192,256},{320,384},{128,64},{256,192},{384,320},{65,129}... | collective-permute-start | bytes 393224 | tf_op jit(solution)/shard_map/ppermute | solution.py:406
  59.7 12.8 %collective-permute-start = (f32[32,8,128]{2,1,0:T(8,128)S(1)}, f32[32,8,128]{2,1,0:T(8,128)S(1)}, u32[]{:S(2)}, u32[]{:S(2)}) collective-permute-start(f32[32,8,128]{2,1,0:T(8,128)S(1)} %get-tuple-element.9), channel_id=1, source_target_pairs={{0,64},{64,0},{1,65},{65,1},{2,66},{66,2},{3,67},{67,3},{4,68},{68... | collective-permute-start | bytes 393224 | tf_op jit(solution)/shard_map/ppermute | solution.py:401
  70.6 5.5 %collective-permute-start.2 = (f32[32,8,128]{2,1,0:T(8,128)S(1)}, f32[32,8,128]{2,1,0:T(8,128)S(1)}, u32[]{:S(2)}, u32[]{:S(2)}) collective-permute-start(f32[32,8,128]{2,1,0:T(8,128)S(1)} %collective-permute-done.1.outer1_ref), channel_id=1, source_target_pairs={{0,64},{64,0},{1,65},{65,1},{2,66},{66,2},{3,67},{67,3},{4,68},{68... | collective-permute-start | bytes 393224 | tf_op jit(solution)/shard_map/ppermute | solution.py:401
  72.5 12.1 %collective-permute-start.3 = (f32[32,8,128]{2,1,0:T(8,128)S(1)}, f32[32,8,128]{2,1,0:T(8,128)S(1)}, u32[]{:S(2)}, u32[]{:S(2)}) collective-permute-start(f32[32,8,128]{2,1,0:T(8,128)S(1)} %collective-permute-done.inner1_ref), channel_id=1, source_target_pairs={{64,128},{192,256},{320,384},{128,64},{256,192},{384,320},{65,129}... | collective-permute-start | bytes 393224 | tf_op jit(solution)/shard_map/ppermute | solution.py:406

commit v3 on v2

--- a/solution.py
+++ b/solution.py
@@ -24,6 +24,12 @@
 
 SLAB = ("zh", "core")
 VEL = ("x", "y", "zl")
+
+MIDDLE = 42
+VEL_ORDER = [MIDDLE] + list(range(1, MIDDLE)) + [0] + list(range(MIDDLE + 1, 64))
+Z_ORDER = list(range(16, 32)) + list(range(16))
+XY_FIRST = 10
+XY_ORDER = list(range(XY_FIRST, 16)) + list(range(XY_FIRST))
 
 
 def rows_and_lanes():
@@ -103,6 +109,9 @@
     for kind, (b0, b1, by, e0, e1, ey) in enumerate(totals):
         for k, v in enumerate((b0, b1, by, zv * b0, e0, e1, ey, zv * e0)):
             out_ref[pl.ds(k * 32 + kind, NY, stride=4), :] = v * QUAD_WEIGHT
+    first, middle = out_ref[pl.ds(0, 4), :], out_ref[pl.ds(4 * MIDDLE, 4), :]
+    out_ref[pl.ds(0, 4), :] = middle
+    out_ref[pl.ds(4 * MIDDLE, 4), :] = first
 
 
 def owner_kernel(parts_ref, links_ref, solid_ref, out_ref):
@@ -124,8 +133,8 @@
 
 def combine_kernel(parts_ref, out_ref):
     rank = lax.axis_index(VEL)
-    kinds = [parts_ref[pl.ds(kind, 32, stride=6), :] for kind in range(6)]
-    m0, q, hp, hm, lx, own = kinds
+    listed = [parts_ref[pl.ds(kind, 32, stride=6), :] for kind in range(6)]
+    m0, q, hp, hm, lx, own = [jnp.concatenate([v[16:], v[:16]]) for v in listed]
     row = lax.broadcasted_iota(jnp.int32, (32, NZ), 0)
     low = jnp.where(row < 4, 0.0, pltpu.roll(lx, 4, 0))
     inner = jnp.where(row >= 28, 0.0, lx)
@@ -240,8 +249,9 @@
 
     @pl.loop(0, 8)
     def _(k):
+        at = lax.rem(2 * k + 16 - XY_FIRST, 16)
         for t in range(9):
-            t0, t1 = got_ref[2 * k, t], got_ref[2 * k + 1, t]
+            t0, t1 = got_ref[at, t], got_ref[at + 1, t]
             first = jnp.where(low_half, t0, pltpu.roll(t1, 4, 0))
             second = jnp.where(low_half, pltpu.roll(t0, 4, 0), t1)
             if t < 7:
@@ -414,13 +424,13 @@
     parts, to_inner, to_outer = call(moments_kernel, ((256, NZ), half, half), (f, links))
     outer1 = to_next_chip(to_outer)
     inner1 = over_chip(to_inner)
-    parts = lax.all_to_all(parts.reshape(64, 4, NZ), VEL, 0, 0, tiled=True)
+    parts = lax.all_to_all(parts.reshape(64, 4, NZ), VEL, 0, 0, tiled=True, axis_index_groups=[VEL_ORDER])
     (owned,) = call(owner_kernel, ((192, NZ),), (parts.reshape(32, 8, NZ), links, solid), limit=LIMIT)
-    owned = lax.all_to_all(owned.reshape(32, 1, 6 * NZ), SLAB + ("zl",), 0, 0, tiled=True)
+    owned = lax.all_to_all(owned.reshape(32, 1, 6 * NZ), SLAB + ("zl",), 0, 0, tiled=True, axis_index_groups=[Z_ORDER])
     outer2 = to_next_chip(inner1)
     inner2 = over_chip(outer1)
     (block,) = call(combine_kernel, ((16, 72, NZ),), (owned.reshape(192, NZ),), limit=LIMIT)
-    got = lax.all_to_all(block, ("x", "y"), 0, 0, tiled=True)
+    got = lax.all_to_all(block, ("x", "y"), 0, 0, tiled=True, axis_index_groups=[XY_ORDER])
     plane = (NY, NZ)
     (out,) = call(
         finish_kernel,

time: 89.8 us -> 85.7 us (0.954)
  starting transfers between devices: 14.4 us -> 26.9 us
  blocking collectives: 50.6 us -> 41 us
  waiting for transfers between devices: 17.5 us -> 10.4 us
    ppermute x2, starting transfers between devices: 6.82 us -> 14.9 us  [to_next_chip(): return lax.ppermute(block, SLAB, pairs + [(b, a) for a, b in pairs])]
    ppermute x2, waiting for transfers between devices: 17.4 us -> 10.4 us  [to_next_chip(): return lax.ppermute(block, SLAB, pairs + [(b, a) for a, b in pairs])]
    all_to_all x1, blocking collectives: 28.9 us -> 24.2 us  [steps(): lax.all_to_all(owned.reshape(32, 1, 6 * NZ), SLAB + ('zl',), 0, 0, tiled=...]
    all_to_all x1, blocking collectives: 21.7 us -> 16.9 us  [steps(): lax.all_to_all(parts.reshape(64, 4, NZ), VEL, 0, 0, tiled=True, axis_inde...]
    all_to_all x1, starting transfers between devices: 3.71 us -> 8.12 us  [steps(): lax.all_to_all(block, ('x', 'y'), 0, 0, tiled=True, axis_index_groups=[XY...]
where the time goes in v3:
time: 85.7 us; the launch traced here: 85.3 us
  blocking collectives  41 us (48%)
  starting transfers between devices  26.9 us (31%)
  waiting for transfers between devices  10.4 us (12%)
  Pallas kernels  6.89 us (8%)
    all_to_all x1, blocking collectives, steps(): lax.all_to_all(owned.reshape(32, 1, 6 * NZ), SLAB + ('zl',), 0, 0, tiled=...  24.2 us
    all_to_all x1, blocking collectives, steps(): lax.all_to_all(parts.reshape(64, 4, NZ), VEL, 0, 0, tiled=True, axis_inde...  16.9 us
    ppermute x2, starting transfers between devices, to_next_chip(): return lax.ppermute(block, SLAB, pairs + [(b, a) for a, b in pairs])  14.9 us
    ppermute x2, waiting for transfers between devices, to_next_chip(): return lax.ppermute(block, SLAB, pairs + [(b, a) for a, b in pairs])  10.4 us
    all_to_all x1, starting transfers between devices, steps(): lax.all_to_all(block, ('x', 'y'), 0, 0, tiled=True, axis_index_groups=[XY...  8.12 us
    pallas_call x4, Pallas kernels, call(): pl.pallas_call(kernel, out_shape=[keep(shape, F32) for shape in out], in_...  6.89 us
    ppermute x2, starting transfers between devices, over_chip(): return lax.ppermute(block, 'core', [(0, 1), (1, 0)])  3.83 us
  transfers between devices with their start and end apart: 5, of which 2 were waited for; matrix products, arithmetic and copies ran while one was open for 0% of the time, Pallas kernels for 0%

profile of v3, /device:TPU:1, one launch (start us, length us, event | category | flops | bytes accessed | tf_op | source)
XLA Modules:
  0.0 85.3 jit_solution(3705883501330182124)
XLA Ops:
  0.0 1.1 %shard_map.37 = (f32[256,128]{1,0:T(8,128)S(1)}, f32[32,8,128]{2,1,0:T(8,128)S(1)}, f32[32,8,128]{2,1,0:T(8,128)S(1)}) custom-call(f32[64,8,128]{2,1,0:T(8,128)} %bitcast.12, s32[3,8,128]{2,1,0:T(8,128)} %bitcast.18), custom_call_target="tpu_custom_call" | custom-call | tf_op jit(solution)/shard_map/pallas_call | solution.py:400
  1.1 0.0 copy-start.1
  1.1 0.0 copy-start.2
  1.1 16.9 %all_to_all.15 = f32[64,4,128]{2,1,0:T(4,128)S(1)} all-to-all(f32[64,4,128]{2,1,0:T(4,128)S(1)} %bitcast.17), channel_id=1, replica_groups={{42,1,2,3,4,5,6,7,8,9,10,11,12,13,14,15,16,17,18,19,20,21,22,23,24,25,2..., dimensions={0} | all-to-all | bytes 262144 | tf_op jit(solution)/shard_map/all_to_all | solution.py:427
  18.0 0.0 copy-done.1
  18.0 0.0 copy-done.2
  18.1 24.2 %all_to_all.16 = f32[32,1,768]{2,1,0:T(1,128)S(1)} all-to-all(f32[32,1,768]{2,1,0:T(1,128)S(1)} %bitcast.15), channel_id=1, replica_groups={{256,257,258,259,320,321,322,323,384,385,386,387,448,449,450,451,0,1,2,..., dimensions={0} | all-to-all | bytes 196608 | tf_op jit(solution)/shard_map/all_to_all | solution.py:429
  42.2 0.9 %shard_map.39 = f32[16,72,128]{2,1,0:T(8,128)} custom-call(f32[192,128]{1,0:T(8,128)S(1)} %bitcast.16), custom_call_target="tpu_custom_call" | custom-call | tf_op jit(solution)/shard_map/pallas_call | solution.py:400
  43.1 0.0 copy-start
  43.1 8.1 %all-to-all-start.2 = ((f32[16,72,128]{2,1,0:T(8,128)}), f32[16,72,128]{2,1,0:T(8,128)S(1)}, u32[]{:S(2)}, u32[]{:S(2)}) async-start(f32[16,72,128]{2,1,0:T(8,128)} %shard_map.39), calls=%async_computation.2 | async-start | bytes 1179648 | tf_op jit(solution)/shard_map/all_to_all | solution.py:433
  51.2 7.6 %collective-permute-start.1 = (f32[32,8,128]{2,1,0:T(8,128)S(1)}, f32[32,8,128]{2,1,0:T(8,128)S(1)}, u32[]{:S(2)}, u32[]{:S(2)}) collective-permute-start(f32[32,8,128]{2,1,0:T(8,128)S(1)} %get-tuple-element.10), channel_id=1, source_target_pairs={{64,128},{192,256},{320,384},{128,64},{256,192},{384,320},{65,129}... | collective-permute-start | bytes 393224 | tf_op jit(solution)/shard_map/ppermute | solution.py:416
  58.9 1.9 %collective-permute-start = (f32[32,8,128]{2,1,0:T(8,128)S(1)}, f32[32,8,128]{2,1,0:T(8,128)S(1)}, u32[]{:S(2)}, u32[]{:S(2)}) collective-permute-start(f32[32,8,128]{2,1,0:T(8,128)S(1)} %get-tuple-element.9), channel_id=1, source_target_pairs={{0,64},{64,0},{1,65},{65,1},{2,66},{66,2},{3,67},{67,3},{4,68},{68... | collective-permute-start | bytes 393224 | tf_op jit(solution)/shard_map/ppermute | solution.py:411
  60.8 4.9 %collective-permute-done.1.outer1_ref = f32[32,8,128]{2,1,0:T(8,128)S(1)} collective-permute-done((f32[32,8,128]{2,1,0:T(8,128)S(1)}, f32[32,8,128]{2,1,0:T(8,128)S(1)}, u32[]{:S(2)}, u32[]{:S(2)}) %collective-permute-start.1) | collective-permute-done | bytes 131104 | tf_op jit(solution)/shard_map/ppermute | solution.py:416
  65.7 1.9 %collective-permute-start.2 = (f32[32,8,128]{2,1,0:T(8,128)S(1)}, f32[32,8,128]{2,1,0:T(8,128)S(1)}, u32[]{:S(2)}, u32[]{:S(2)}) collective-permute-start(f32[32,8,128]{2,1,0:T(8,128)S(1)} %collective-permute-done.1.outer1_ref), channel_id=1, source_target_pairs={{0,64},{64,0},{1,65},{65,1},{2,66},{66,2},{3,67},{67,3},{4,68},{68... | collective-permute-start | bytes 393224 | tf_op jit(solution)/shard_map/ppermute | solution.py:411
  67.6 0.0 collective-permute-done.inner1_ref
  67.6 7.3 %collective-permute-start.3 = (f32[32,8,128]{2,1,0:T(8,128)S(1)}, f32[32,8,128]{2,1,0:T(8,128)S(1)}, u32[]{:S(2)}, u32[]{:S(2)}) collective-permute-start(f32[32,8,128]{2,1,0:T(8,128)S(1)} %collective-permute-done.inner1_ref), channel_id=1, source_target_pairs={{64,128},{192,256},{320,384},{128,64},{256,192},{384,320},{65,129}... | collective-permute-start | bytes 393224 | tf_op jit(solution)/shard_map/ppermute | solution.py:416
  75.0 0.0 collective-permute-done.2.inner2_ref
  75.0 5.4 %collective-permute-done.3.outer2_ref = f32[32,8,128]{2,1,0:T(8,128)S(1)} collective-permute-done((f32[32,8,128]{2,1,0:T(8,128)S(1)}, f32[32,8,128]{2,1,0:T(8,128)S(1)}, u32[]{:S(2)}, u32[]{:S(2)}) %collective-permute-start.3) | collective-permute-done | bytes 131104 | tf_op jit(solution)/shard_map/ppermute | solution.py:416
  80.4 0.0 all-to-all-done.2
  80.4 0.0 copy-done
  80.4 4.9 %shard_map.40 = f32[64,8,128]{2,1,0:T(8,128)} custom-call(f32[16,9,8,128]{3,2,1,0:T(8,128)S(1)} %bitcast.11, f32[64,8,128]{2,1,0:T(8,128)S(1)} %bitcast.13, f32[32,8,128]{2,1,0:T(8,128)S(1)} %collective-permute-done.inner1_ref, f32[32,8,128]{2,1,0:T(8,128)S(1)} %collective-permute-done.2.inner2_ref, f32[32,8,128]{2,1,0:T(8,128)S(1)} %collective-permute-done.1.outer1_ref, ...), custom_call_target="tpu_custom_call" | custom-call | tf_op jit(solution)/shard_map/pallas_call | solution.py:400
  (1 shorter events, 0.0 us)
Async XLA Ops:
  1.1 16.9 %copy-start.1 = (s32[3,1,8,128]{3,2,1,0:T(8,128)S(1)}, s32[3,1,8,128]{3,2,1,0:T(8,128)}, u32[]{:S(2)}) copy-start(s32[3,1,8,128]{3,2,1,0:T(8,128)} %param.4) | copy-start | bytes 36868
  1.1 16.9 %copy-start.2 = (s32[1,8,128]{2,1,0:T(8,128)S(1)}, s32[1,8,128]{2,1,0:T(8,128)}, u32[]{:S(2)}) copy-start(s32[1,8,128]{2,1,0:T(8,128)} %param.5) | copy-start | bytes 12292
  43.1 37.3 %copy-start = (f32[64,1,8,128]{3,2,1,0:T(8,128)S(1)}, f32[64,1,8,128]{3,2,1,0:T(8,128)}, u32[]{:S(2)}) copy-start(f32[64,1,8,128]{3,2,1,0:T(8,128)} %param.3) | copy-start | bytes 786436
  43.1 37.3 %all-to-all-start.2 = ((f32[16,72,128]{2,1,0:T(8,128)}), f32[16,72,128]{2,1,0:T(8,128)S(1)}, u32[]{:S(2)}, u32[]{:S(2)}) async-start(f32[16,72,128]{2,1,0:T(8,128)} %shard_map.39), calls=%async_computation.2 | async-start | bytes 1179648 | tf_op jit(solution)/shard_map/all_to_all | solution.py:433
  51.2 14.5 %collective-permute-start.1 = (f32[32,8,128]{2,1,0:T(8,128)S(1)}, f32[32,8,128]{2,1,0:T(8,128)S(1)}, u32[]{:S(2)}, u32[]{:S(2)}) collective-permute-start(f32[32,8,128]{2,1,0:T(8,128)S(1)} %get-tuple-element.10), channel_id=1, source_target_pairs={{64,128},{192,256},{320,384},{128,64},{256,192},{384,320},{65,129}... | collective-permute-start | bytes 393224 | tf_op jit(solution)/shard_map/ppermute | solution.py:416
  58.9 8.8 %collective-permute-start = (f32[32,8,128]{2,1,0:T(8,128)S(1)}, f32[32,8,128]{2,1,0:T(8,128)S(1)}, u32[]{:S(2)}, u32[]{:S(2)}) collective-permute-start(f32[32,8,128]{2,1,0:T(8,128)S(1)} %get-tuple-element.9), channel_id=1, source_target_pairs={{0,64},{64,0},{1,65},{65,1},{2,66},{66,2},{3,67},{67,3},{4,68},{68... | collective-permute-start | bytes 393224 | tf_op jit(solution)/shard_map/ppermute | solution.py:411
  65.7 9.3 %collective-permute-start.2 = (f32[32,8,128]{2,1,0:T(8,128)S(1)}, f32[32,8,128]{2,1,0:T(8,128)S(1)}, u32[]{:S(2)}, u32[]{:S(2)}) collective-permute-start(f32[32,8,128]{2,1,0:T(8,128)S(1)} %collective-permute-done.1.outer1_ref), channel_id=1, source_target_pairs={{0,64},{64,0},{1,65},{65,1},{2,66},{66,2},{3,67},{67,3},{4,68},{68... | collective-permute-start | bytes 393224 | tf_op jit(solution)/shard_map/ppermute | solution.py:411
  67.6 12.8 %collective-permute-start.3 = (f32[32,8,128]{2,1,0:T(8,128)S(1)}, f32[32,8,128]{2,1,0:T(8,128)S(1)}, u32[]{:S(2)}, u32[]{:S(2)}) collective-permute-start(f32[32,8,128]{2,1,0:T(8,128)S(1)} %collective-permute-done.inner1_ref), channel_id=1, source_target_pairs={{64,128},{192,256},{320,384},{128,64},{256,192},{384,320},{65,129}... | collective-permute-start | bytes 393224 | tf_op jit(solution)/shard_map/ppermute | solution.py:416

commit v4 on v3

--- a/solution.py
+++ b/solution.py
@@ -168,18 +168,28 @@
 
 
 def target_moments(u, u2, inv_t, s, height):
-    half_t = -0.5 * inv_t
+    half_t = (-0.5 * math.log2(math.e)) * inv_t
     one_d = []
     for a in range(3):
-        m = [None] * 7
-        for i in range(NQ):
-            c = xi(i) - u[a]
-            t = jnp.exp(c * c * half_t)
-            for n in range(7):
-                m[n] = t if m[n] is None else m[n] + t
-                if n < 6:
-                    t = t * c
-        one_d.append(m)
+        even, odd = [None] * 4, [None] * 3
+        for j in range(HALF):
+            d = (j + 0.5) * SPACING
+            sides = []
+            for c in (-d - u[a], d - u[a]):
+                c2 = c * c
+                levels = [jnp.exp2(c2 * half_t)]
+                for _ in range(3):
+                    levels.append(levels[-1] * c2)
+                sides.append(levels)
+            below, above = sides
+            for n in range(4):
+                t = below[n] + above[n]
+                even[n] = t if even[n] is None else even[n] + t
+            for n in range(3):
+                t = d * (above[n] - below[n])
+                odd[n] = t if odd[n] is None else odd[n] + t
+        odd = [t - u[a] * e for t, e in zip(odd, even)]
+        one_d.append([even[0], odd[0], even[1], odd[1], even[2], odd[2], even[3]])
     x, y, z = one_d
     made = {}
 
@@ -236,7 +246,7 @@
 
 def finish_kernel(
     got_ref, f_ref, inner1_ref, inner2_ref, outer1_ref, outer2_ref, out_ref, m_ref, l_ref, w_ref, pred_ref, next_ref,
-    xe_ref, xc_ref, f1_ref, h1_ref,
+    xe_ref, xc_ref, xs_ref, xo_ref, xn_ref, f1_ref, h1_ref,
 ):
     rank, slab, core = lax.axis_index(VEL), lax.axis_index(SLAB), lax.axis_index("core")
     row, lane = rows_and_lanes()
@@ -279,7 +289,7 @@
         w_ref[5, s + 1] = share * lz_low
         w_ref[6, s + 1] = share
 
-    @pl.loop(0, 8)
+    @pl.loop(0, 8, unroll=2)
     def _(k):
         start = [m_ref[0, k, s] for s in range(NS)]
         now = start
@@ -334,12 +344,6 @@
     def advance(planes, here, halves, source, beside, sink):
         u, _, inv_t, nu, s, height = macro_state(planes)
         half_t = -0.5 * inv_t
-        for i in range(NQ):
-            if i // HALF in halves:
-                c = xi(i) - u[0]
-                c2 = c * c
-                xe_ref[i] = jnp.exp(c2 * half_t)
-                xc_ref[i] = c2 * inv_t
         share = 1.0 / (1.0 + nu)
         lx, lx_low = l_ref[0, here + 1], l_ref[0, here]
         lx_in = jnp.where(here < NS - 1, lx, 0.0)
@@ -351,15 +355,25 @@
         cz = zv - u[2]
         out_x = (move * lx_low, move * lx)
         in_x = (move * lx_in, move * lx_low)
-
-        @pl.loop(0, LY)
+        for i in range(NQ):
+            side = i // HALF
+            if side in halves:
+                c = xi(i) - u[0]
+                c2 = c * c
+                xe_ref[i] = jnp.exp(c2 * half_t)
+                xc_ref[i] = c2 * inv_t
+                xs_ref[i] = c * s[0]
+                xo_ref[i] = abs(xi(i)) * out_x[side]
+                xn_ref[i] = abs(xi(i)) * in_x[side]
+
+        @pl.loop(0, LY, unroll=2 if len(halves) == 1 else 1)
         def _(jy):
             yv = speed_of(rank % 4 * LY + jy)
             ay = COURANT * jnp.abs(yv)
             cy = yv - u[1]
             c2 = cy * cy + cz * cz
             top = nu * share * height * jnp.exp(c2 * half_t)
-            tilt = cy * s[1] + cz * s[2] - u[0] * s[0]
+            tilt = cy * s[1] + cz * s[2]
             lift = c2 * inv_t - 5.0
             keep = share * (1.0 - ay * out_y - az * out_z)
             from_y = ay * share * in_y
@@ -367,9 +381,8 @@
                 side = i // HALF
                 if side in halves:
                     f = source(jy, i)
-                    a = abs(xi(i))
-                    goal = top * xe_ref[i] * (1.0 + (xi(i) * s[0] + tilt) * (xc_ref[i] + lift))
-                    fresh = f * (keep - a * out_x[side]) + (a * in_x[side]) * beside(jy, i)
+                    goal = top * xe_ref[i] * (1.0 + (xs_ref[i] + tilt) * (xc_ref[i] + lift))
+                    fresh = f * (keep - xo_ref[i]) + xn_ref[i] * beside(jy, i)
                     fresh = fresh + from_y * pltpu.roll(f, shift_y, 0) + in_z * pltpu.roll(f, shift_z, 1)
                     sink[jy * NQ + i] = jnp.where(body, f, fresh + goal)
 
@@ -444,6 +457,9 @@
             (8, NS + 4) + plane,
             (NQ,) + plane,
             (NQ,) + plane,
+            (NQ,) + plane,
+            (NQ,) + plane,
+            (NQ,) + plane,
             f.shape,
             f.shape,
         ),

time: 85.7 us -> 84.7 us (0.988)
  Pallas kernels: 6.89 us -> 5.95 us
    pallas_call x4, Pallas kernels: 6.89 us -> 5.95 us  [call(): pl.pallas_call(kernel, out_shape=[keep(shape, F32) for shape in out], in_...]
where the time goes in v4:
time: 84.7 us; the launch traced here: 84.3 us
  blocking collectives  41 us (48%)
  starting transfers between devices  26.9 us (32%)
  waiting for transfers between devices  10.4 us (12%)
  Pallas kernels  5.95 us (7%)
    all_to_all x1, blocking collectives, steps(): lax.all_to_all(owned.reshape(32, 1, 6 * NZ), SLAB + ('zl',), 0, 0, tiled=...  24.2 us
    all_to_all x1, blocking collectives, steps(): lax.all_to_all(parts.reshape(64, 4, NZ), VEL, 0, 0, tiled=True, axis_inde...  16.9 us
    ppermute x2, starting transfers between devices, to_next_chip(): return lax.ppermute(block, SLAB, pairs + [(b, a) for a, b in pairs])  14.9 us
    ppermute x2, waiting for transfers between devices, to_next_chip(): return lax.ppermute(block, SLAB, pairs + [(b, a) for a, b in pairs])  10.4 us
    all_to_all x1, starting transfers between devices, steps(): lax.all_to_all(block, ('x', 'y'), 0, 0, tiled=True, axis_index_groups=[XY...  8.12 us
    pallas_call x4, Pallas kernels, call(): pl.pallas_call(kernel, out_shape=[keep(shape, F32) for shape in out], in_...  5.95 us
    ppermute x2, starting transfers between devices, over_chip(): return lax.ppermute(block, 'core', [(0, 1), (1, 0)])  3.83 us
  transfers between devices with their start and end apart: 5, of which 2 were waited for; matrix products, arithmetic and copies ran while one was open for 0% of the time, Pallas kernels for 0%

profile of v4, /device:TPU:1, one launch (start us, length us, event | category | flops | bytes accessed | tf_op | source)
XLA Modules:
  0.0 84.3 jit_solution(10038241103522986123)
XLA Ops:
  0.0 1.1 %shard_map.37 = (f32[256,128]{1,0:T(8,128)S(1)}, f32[32,8,128]{2,1,0:T(8,128)S(1)}, f32[32,8,128]{2,1,0:T(8,128)S(1)}) custom-call(f32[64,8,128]{2,1,0:T(8,128)} %bitcast.12, s32[3,8,128]{2,1,0:T(8,128)} %bitcast.18), custom_call_target="tpu_custom_call" | custom-call | tf_op jit(solution)/shard_map/pallas_call | solution.py:413
  1.1 0.0 copy-start.1
  1.1 0.0 copy-start.2
  1.1 16.9 %all_to_all.15 = f32[64,4,128]{2,1,0:T(4,128)S(1)} all-to-all(f32[64,4,128]{2,1,0:T(4,128)S(1)} %bitcast.17), channel_id=1, replica_groups={{42,1,2,3,4,5,6,7,8,9,10,11,12,13,14,15,16,17,18,19,20,21,22,23,24,25,2..., dimensions={0} | all-to-all | bytes 262144 | tf_op jit(solution)/shard_map/all_to_all | solution.py:440
  18.0 0.0 copy-done.1
  18.0 0.0 copy-done.2
  18.1 24.2 %all_to_all.16 = f32[32,1,768]{2,1,0:T(1,128)S(1)} all-to-all(f32[32,1,768]{2,1,0:T(1,128)S(1)} %bitcast.15), channel_id=1, replica_groups={{256,257,258,259,320,321,322,323,384,385,386,387,448,449,450,451,0,1,2,..., dimensions={0} | all-to-all | bytes 196608 | tf_op jit(solution)/shard_map/all_to_all | solution.py:442
  42.2 0.9 %shard_map.39 = f32[16,72,128]{2,1,0:T(8,128)} custom-call(f32[192,128]{1,0:T(8,128)S(1)} %bitcast.16), custom_call_target="tpu_custom_call" | custom-call | tf_op jit(solution)/shard_map/pallas_call | solution.py:413
  43.1 0.0 copy-start
  43.1 8.1 %all-to-all-start.2 = ((f32[16,72,128]{2,1,0:T(8,128)}), f32[16,72,128]{2,1,0:T(8,128)S(1)}, u32[]{:S(2)}, u32[]{:S(2)}) async-start(f32[16,72,128]{2,1,0:T(8,128)} %shard_map.39), calls=%async_computation.2 | async-start | bytes 1179648 | tf_op jit(solution)/shard_map/all_to_all | solution.py:446
  51.2 7.6 %collective-permute-start.1 = (f32[32,8,128]{2,1,0:T(8,128)S(1)}, f32[32,8,128]{2,1,0:T(8,128)S(1)}, u32[]{:S(2)}, u32[]{:S(2)}) collective-permute-start(f32[32,8,128]{2,1,0:T(8,128)S(1)} %get-tuple-element.10), channel_id=1, source_target_pairs={{64,128},{192,256},{320,384},{128,64},{256,192},{384,320},{65,129}... | collective-permute-start | bytes 393224 | tf_op jit(solution)/shard_map/ppermute | solution.py:429
  58.9 1.9 %collective-permute-start = (f32[32,8,128]{2,1,0:T(8,128)S(1)}, f32[32,8,128]{2,1,0:T(8,128)S(1)}, u32[]{:S(2)}, u32[]{:S(2)}) collective-permute-start(f32[32,8,128]{2,1,0:T(8,128)S(1)} %get-tuple-element.9), channel_id=1, source_target_pairs={{0,64},{64,0},{1,65},{65,1},{2,66},{66,2},{3,67},{67,3},{4,68},{68... | collective-permute-start | bytes 393224 | tf_op jit(solution)/shard_map/ppermute | solution.py:424
  60.8 4.9 %collective-permute-done.1.outer1_ref = f32[32,8,128]{2,1,0:T(8,128)S(1)} collective-permute-done((f32[32,8,128]{2,1,0:T(8,128)S(1)}, f32[32,8,128]{2,1,0:T(8,128)S(1)}, u32[]{:S(2)}, u32[]{:S(2)}) %collective-permute-start.1) | collective-permute-done | bytes 131104 | tf_op jit(solution)/shard_map/ppermute | solution.py:429
  65.7 1.9 %collective-permute-start.2 = (f32[32,8,128]{2,1,0:T(8,128)S(1)}, f32[32,8,128]{2,1,0:T(8,128)S(1)}, u32[]{:S(2)}, u32[]{:S(2)}) collective-permute-start(f32[32,8,128]{2,1,0:T(8,128)S(1)} %collective-permute-done.1.outer1_ref), channel_id=1, source_target_pairs={{0,64},{64,0},{1,65},{65,1},{2,66},{66,2},{3,67},{67,3},{4,68},{68... | collective-permute-start | bytes 393224 | tf_op jit(solution)/shard_map/ppermute | solution.py:424
  67.6 0.0 collective-permute-done.inner1_ref
  67.6 7.3 %collective-permute-start.3 = (f32[32,8,128]{2,1,0:T(8,128)S(1)}, f32[32,8,128]{2,1,0:T(8,128)S(1)}, u32[]{:S(2)}, u32[]{:S(2)}) collective-permute-start(f32[32,8,128]{2,1,0:T(8,128)S(1)} %collective-permute-done.inner1_ref), channel_id=1, source_target_pairs={{64,128},{192,256},{320,384},{128,64},{256,192},{384,320},{65,129}... | collective-permute-start | bytes 393224 | tf_op jit(solution)/shard_map/ppermute | solution.py:429
  75.0 0.0 collective-permute-done.2.inner2_ref
  75.0 5.4 %collective-permute-done.3.outer2_ref = f32[32,8,128]{2,1,0:T(8,128)S(1)} collective-permute-done((f32[32,8,128]{2,1,0:T(8,128)S(1)}, f32[32,8,128]{2,1,0:T(8,128)S(1)}, u32[]{:S(2)}, u32[]{:S(2)}) %collective-permute-start.3) | collective-permute-done | bytes 131104 | tf_op jit(solution)/shard_map/ppermute | solution.py:429
  80.4 0.0 all-to-all-done.2
  80.4 0.0 copy-done
  80.4 3.9 %shard_map.40 = f32[64,8,128]{2,1,0:T(8,128)} custom-call(f32[16,9,8,128]{3,2,1,0:T(8,128)S(1)} %bitcast.11, f32[64,8,128]{2,1,0:T(8,128)S(1)} %bitcast.13, f32[32,8,128]{2,1,0:T(8,128)S(1)} %collective-permute-done.inner1_ref, f32[32,8,128]{2,1,0:T(8,128)S(1)} %collective-permute-done.2.inner2_ref, f32[32,8,128]{2,1,0:T(8,128)S(1)} %collective-permute-done.1.outer1_ref, ...), custom_call_target="tpu_custom_call" | custom-call | tf_op jit(solution)/shard_map/pallas_call | solution.py:413
  (1 shorter events, 0.0 us)
Async XLA Ops:
  1.1 16.9 %copy-start.1 = (s32[3,1,8,128]{3,2,1,0:T(8,128)S(1)}, s32[3,1,8,128]{3,2,1,0:T(8,128)}, u32[]{:S(2)}) copy-start(s32[3,1,8,128]{3,2,1,0:T(8,128)} %param.4) | copy-start | bytes 36868
  1.1 16.9 %copy-start.2 = (s32[1,8,128]{2,1,0:T(8,128)S(1)}, s32[1,8,128]{2,1,0:T(8,128)}, u32[]{:S(2)}) copy-start(s32[1,8,128]{2,1,0:T(8,128)} %param.5) | copy-start | bytes 12292
  43.1 37.3 %copy-start = (f32[64,1,8,128]{3,2,1,0:T(8,128)S(1)}, f32[64,1,8,128]{3,2,1,0:T(8,128)}, u32[]{:S(2)}) copy-start(f32[64,1,8,128]{3,2,1,0:T(8,128)} %param.3) | copy-start | bytes 786436
  43.1 37.3 %all-to-all-start.2 = ((f32[16,72,128]{2,1,0:T(8,128)}), f32[16,72,128]{2,1,0:T(8,128)S(1)}, u32[]{:S(2)}, u32[]{:S(2)}) async-start(f32[16,72,128]{2,1,0:T(8,128)} %shard_map.39), calls=%async_computation.2 | async-start | bytes 1179648 | tf_op jit(solution)/shard_map/all_to_all | solution.py:446
  51.2 14.5 %collective-permute-start.1 = (f32[32,8,128]{2,1,0:T(8,128)S(1)}, f32[32,8,128]{2,1,0:T(8,128)S(1)}, u32[]{:S(2)}, u32[]{:S(2)}) collective-permute-start(f32[32,8,128]{2,1,0:T(8,128)S(1)} %get-tuple-element.10), channel_id=1, source_target_pairs={{64,128},{192,256},{320,384},{128,64},{256,192},{384,320},{65,129}... | collective-permute-start | bytes 393224 | tf_op jit(solution)/shard_map/ppermute | solution.py:429
  58.9 8.8 %collective-permute-start = (f32[32,8,128]{2,1,0:T(8,128)S(1)}, f32[32,8,128]{2,1,0:T(8,128)S(1)}, u32[]{:S(2)}, u32[]{:S(2)}) collective-permute-start(f32[32,8,128]{2,1,0:T(8,128)S(1)} %get-tuple-element.9), channel_id=1, source_target_pairs={{0,64},{64,0},{1,65},{65,1},{2,66},{66,2},{3,67},{67,3},{4,68},{68... | collective-permute-start | bytes 393224 | tf_op jit(solution)/shard_map/ppermute | solution.py:424
  65.7 9.3 %collective-permute-start.2 = (f32[32,8,128]{2,1,0:T(8,128)S(1)}, f32[32,8,128]{2,1,0:T(8,128)S(1)}, u32[]{:S(2)}, u32[]{:S(2)}) collective-permute-start(f32[32,8,128]{2,1,0:T(8,128)S(1)} %collective-permute-done.1.outer1_ref), channel_id=1, source_target_pairs={{0,64},{64,0},{1,65},{65,1},{2,66},{66,2},{3,67},{67,3},{4,68},{68... | collective-permute-start | bytes 393224 | tf_op jit(solution)/shard_map/ppermute | solution.py:424
  67.6 12.8 %collective-permute-start.3 = (f32[32,8,128]{2,1,0:T(8,128)S(1)}, f32[32,8,128]{2,1,0:T(8,128)S(1)}, u32[]{:S(2)}, u32[]{:S(2)}) collective-permute-start(f32[32,8,128]{2,1,0:T(8,128)S(1)} %collective-permute-done.inner1_ref), channel_id=1, source_target_pairs={{64,128},{192,256},{320,384},{128,64},{256,192},{384,320},{65,129}... | collective-permute-start | bytes 393224 | tf_op jit(solution)/shard_map/ppermute | solution.py:429

commit v5 on v4

--- a/solution.py
+++ b/solution.py
@@ -27,9 +27,9 @@
 
 MIDDLE = 42
 VEL_ORDER = [MIDDLE] + list(range(1, MIDDLE)) + [0] + list(range(MIDDLE + 1, 64))
-Z_ORDER = list(range(16, 32)) + list(range(16))
+Z_ORDER = [16] + list(range(16)) + list(range(17, 32))
 XY_FIRST = 10
-XY_ORDER = list(range(XY_FIRST, 16)) + list(range(XY_FIRST))
+XY_ORDER = [XY_FIRST] + list(range(XY_FIRST)) + list(range(XY_FIRST + 1, 16))
 
 
 def rows_and_lanes():
@@ -134,8 +134,10 @@
 def combine_kernel(parts_ref, out_ref):
     rank = lax.axis_index(VEL)
     listed = [parts_ref[pl.ds(kind, 32, stride=6), :] for kind in range(6)]
-    m0, q, hp, hm, lx, own = [jnp.concatenate([v[16:], v[:16]]) for v in listed]
     row = lax.broadcasted_iota(jnp.int32, (32, NZ), 0)
+    m0, q, hp, hm, lx, own = [
+        jnp.where(row < 16, pltpu.roll(v, 31, 0), jnp.where(row == 16, pltpu.roll(v, 16, 0), v)) for v in listed
+    ]
     low = jnp.where(row < 4, 0.0, pltpu.roll(lx, 4, 0))
     inner = jnp.where(row >= 28, 0.0, lx)
     mt = q - COURANT * (lx * hp + low * hm - low * pltpu.roll(hp, 4, 0) - inner * pltpu.roll(hm, 28, 0))
@@ -259,9 +261,10 @@
 
     @pl.loop(0, 8)
     def _(k):
-        at = lax.rem(2 * k + 16 - XY_FIRST, 16)
+        at = jnp.where(2 * k == XY_FIRST, 0, jnp.where(k < XY_FIRST // 2, 2 * k + 1, 2 * k))
+        beside = jnp.where(k < XY_FIRST // 2, 2 * k + 2, 2 * k + 1)
         for t in range(9):
-            t0, t1 = got_ref[at, t], got_ref[at + 1, t]
+            t0, t1 = got_ref[at, t], got_ref[beside, t]
             first = jnp.where(low_half, t0, pltpu.roll(t1, 4, 0))
             second = jnp.where(low_half, pltpu.roll(t0, 4, 0), t1)
             if t < 7:

time: 84.7 us -> 84.1 us (level)
  starting transfers between devices: 26.9 us -> 24.7 us
  waiting for transfers between devices: 10.4 us -> 11.9 us
    ppermute x2, starting transfers between devices: 14.9 us -> 12.8 us  [to_next_chip(): return lax.ppermute(block, SLAB, pairs + [(b, a) for a, b in pairs])]
    ppermute x2, waiting for transfers between devices: 10.4 us -> 11.9 us  [to_next_chip(): return lax.ppermute(block, SLAB, pairs + [(b, a) for a, b in pairs])]
where the time goes in v5:
time: 84.1 us; the launch traced here: 83.7 us
  blocking collectives  41.1 us (49%)
  starting transfers between devices  24.7 us (29%)
  waiting for transfers between devices  11.9 us (14%)
  Pallas kernels  5.95 us (7%)
    all_to_all x1, blocking collectives, steps(): lax.all_to_all(owned.reshape(32, 1, 6 * NZ), SLAB + ('zl',), 0, 0, tiled=...  24.2 us
    all_to_all x1, blocking collectives, steps(): lax.all_to_all(parts.reshape(64, 4, NZ), VEL, 0, 0, tiled=True, axis_inde...  16.9 us
    ppermute x2, starting transfers between devices, to_next_chip(): return lax.ppermute(block, SLAB, pairs + [(b, a) for a, b in pairs])  12.8 us
    ppermute x2, waiting for transfers between devices, to_next_chip(): return lax.ppermute(block, SLAB, pairs + [(b, a) for a, b in pairs])  11.9 us
    all_to_all x1, starting transfers between devices, steps(): lax.all_to_all(block, ('x', 'y'), 0, 0, tiled=True, axis_index_groups=[XY...  8.09 us
    pallas_call x4, Pallas kernels, call(): pl.pallas_call(kernel, out_shape=[keep(shape, F32) for shape in out], in_...  5.95 us
    ppermute x2, starting transfers between devices, over_chip(): return lax.ppermute(block, 'core', [(0, 1), (1, 0)])  3.83 us
  transfers between devices with their start and end apart: 5, of which 2 were waited for; matrix products, arithmetic and copies ran while one was open for 0% of the time, Pallas kernels for 0%

profile of v5, /device:TPU:1, one launch (start us, length us, event | category | flops | bytes accessed | tf_op | source)
XLA Modules:
  0.0 83.7 jit_solution(5141965007053012417)
XLA Ops:
  0.0 1.1 %shard_map.37 = (f32[256,128]{1,0:T(8,128)S(1)}, f32[32,8,128]{2,1,0:T(8,128)S(1)}, f32[32,8,128]{2,1,0:T(8,128)S(1)}) custom-call(f32[64,8,128]{2,1,0:T(8,128)} %bitcast.12, s32[3,8,128]{2,1,0:T(8,128)} %bitcast.18), custom_call_target="tpu_custom_call" | custom-call | tf_op jit(solution)/shard_map/pallas_call | solution.py:416
  1.1 0.0 copy-start.1
  1.1 0.0 copy-start.2
  1.1 16.9 %all_to_all.15 = f32[64,4,128]{2,1,0:T(4,128)S(1)} all-to-all(f32[64,4,128]{2,1,0:T(4,128)S(1)} %bitcast.17), channel_id=1, replica_groups={{42,1,2,3,4,5,6,7,8,9,10,11,12,13,14,15,16,17,18,19,20,21,22,23,24,25,2..., dimensions={0} | all-to-all | bytes 262144 | tf_op jit(solution)/shard_map/all_to_all | solution.py:443
  18.0 0.0 copy-done.1
  18.0 0.0 copy-done.2
  18.1 24.2 %all_to_all.16 = f32[32,1,768]{2,1,0:T(1,128)S(1)} all-to-all(f32[32,1,768]{2,1,0:T(1,128)S(1)} %bitcast.15), channel_id=1, replica_groups={{256,0,1,2,3,64,65,66,67,128,129,130,131,192,193,194,195,257,258,259,32..., dimensions={0} | all-to-all | bytes 196608 | tf_op jit(solution)/shard_map/all_to_all | solution.py:445
  42.3 0.9 %shard_map.39 = f32[16,72,128]{2,1,0:T(8,128)} custom-call(f32[192,128]{1,0:T(8,128)S(1)} %bitcast.16), custom_call_target="tpu_custom_call" | custom-call | tf_op jit(solution)/shard_map/pallas_call | solution.py:416
  43.1 0.0 copy-start
  43.1 8.1 %all-to-all-start.2 = ((f32[16,72,128]{2,1,0:T(8,128)}), f32[16,72,128]{2,1,0:T(8,128)S(1)}, u32[]{:S(2)}, u32[]{:S(2)}) async-start(f32[16,72,128]{2,1,0:T(8,128)} %shard_map.39), calls=%async_computation.2 | async-start | bytes 1179648 | tf_op jit(solution)/shard_map/all_to_all | solution.py:449
  51.2 7.7 %collective-permute-start.1 = (f32[32,8,128]{2,1,0:T(8,128)S(1)}, f32[32,8,128]{2,1,0:T(8,128)S(1)}, u32[]{:S(2)}, u32[]{:S(2)}) collective-permute-start(f32[32,8,128]{2,1,0:T(8,128)S(1)} %get-tuple-element.10), channel_id=1, source_target_pairs={{64,128},{192,256},{320,384},{128,64},{256,192},{384,320},{65,129}... | collective-permute-start | bytes 393224 | tf_op jit(solution)/shard_map/ppermute | solution.py:432
  58.9 1.9 %collective-permute-start = (f32[32,8,128]{2,1,0:T(8,128)S(1)}, f32[32,8,128]{2,1,0:T(8,128)S(1)}, u32[]{:S(2)}, u32[]{:S(2)}) collective-permute-start(f32[32,8,128]{2,1,0:T(8,128)S(1)} %get-tuple-element.9), channel_id=1, source_target_pairs={{0,64},{64,0},{1,65},{65,1},{2,66},{66,2},{3,67},{67,3},{4,68},{68... | collective-permute-start | bytes 393224 | tf_op jit(solution)/shard_map/ppermute | solution.py:427
  60.9 4.2 %collective-permute-done.1.outer1_ref = f32[32,8,128]{2,1,0:T(8,128)S(1)} collective-permute-done((f32[32,8,128]{2,1,0:T(8,128)S(1)}, f32[32,8,128]{2,1,0:T(8,128)S(1)}, u32[]{:S(2)}, u32[]{:S(2)}) %collective-permute-start.1) | collective-permute-done | bytes 131104 | tf_op jit(solution)/shard_map/ppermute | solution.py:432
  65.1 1.9 %collective-permute-start.2 = (f32[32,8,128]{2,1,0:T(8,128)S(1)}, f32[32,8,128]{2,1,0:T(8,128)S(1)}, u32[]{:S(2)}, u32[]{:S(2)}) collective-permute-start(f32[32,8,128]{2,1,0:T(8,128)S(1)} %collective-permute-done.1.outer1_ref), channel_id=1, source_target_pairs={{0,64},{64,0},{1,65},{65,1},{2,66},{66,2},{3,67},{67,3},{4,68},{68... | collective-permute-start | bytes 393224 | tf_op jit(solution)/shard_map/ppermute | solution.py:427
  67.0 0.0 collective-permute-done.inner1_ref
  67.0 5.1 %collective-permute-start.3 = (f32[32,8,128]{2,1,0:T(8,128)S(1)}, f32[32,8,128]{2,1,0:T(8,128)S(1)}, u32[]{:S(2)}, u32[]{:S(2)}) collective-permute-start(f32[32,8,128]{2,1,0:T(8,128)S(1)} %collective-permute-done.inner1_ref), channel_id=1, source_target_pairs={{64,128},{192,256},{320,384},{128,64},{256,192},{384,320},{65,129}... | collective-permute-start | bytes 393224 | tf_op jit(solution)/shard_map/ppermute | solution.py:432
  72.1 0.0 collective-permute-done.2.inner2_ref
  72.1 7.7 %collective-permute-done.3.outer2_ref = f32[32,8,128]{2,1,0:T(8,128)S(1)} collective-permute-done((f32[32,8,128]{2,1,0:T(8,128)S(1)}, f32[32,8,128]{2,1,0:T(8,128)S(1)}, u32[]{:S(2)}, u32[]{:S(2)}) %collective-permute-start.3) | collective-permute-done | bytes 131104 | tf_op jit(solution)/shard_map/ppermute | solution.py:432
  79.8 0.0 all-to-all-done.2
  79.8 0.0 copy-done
  79.8 3.9 %shard_map.40 = f32[64,8,128]{2,1,0:T(8,128)} custom-call(f32[16,9,8,128]{3,2,1,0:T(8,128)S(1)} %bitcast.11, f32[64,8,128]{2,1,0:T(8,128)S(1)} %bitcast.13, f32[32,8,128]{2,1,0:T(8,128)S(1)} %collective-permute-done.inner1_ref, f32[32,8,128]{2,1,0:T(8,128)S(1)} %collective-permute-done.2.inner2_ref, f32[32,8,128]{2,1,0:T(8,128)S(1)} %collective-permute-done.1.outer1_ref, ...), custom_call_target="tpu_custom_call" | custom-call | tf_op jit(solution)/shard_map/pallas_call | solution.py:416
  (1 shorter events, 0.0 us)
Async XLA Ops:
  1.1 16.9 %copy-start.1 = (s32[3,1,8,128]{3,2,1,0:T(8,128)S(1)}, s32[3,1,8,128]{3,2,1,0:T(8,128)}, u32[]{:S(2)}) copy-start(s32[3,1,8,128]{3,2,1,0:T(8,128)} %param.4) | copy-start | bytes 36868
  1.1 16.9 %copy-start.2 = (s32[1,8,128]{2,1,0:T(8,128)S(1)}, s32[1,8,128]{2,1,0:T(8,128)}, u32[]{:S(2)}) copy-start(s32[1,8,128]{2,1,0:T(8,128)} %param.5) | copy-start | bytes 12292
  43.1 36.7 %copy-start = (f32[64,1,8,128]{3,2,1,0:T(8,128)S(1)}, f32[64,1,8,128]{3,2,1,0:T(8,128)}, u32[]{:S(2)}) copy-start(f32[64,1,8,128]{3,2,1,0:T(8,128)} %param.3) | copy-start | bytes 786436
  43.1 36.7 %all-to-all-start.2 = ((f32[16,72,128]{2,1,0:T(8,128)}), f32[16,72,128]{2,1,0:T(8,128)S(1)}, u32[]{:S(2)}, u32[]{:S(2)}) async-start(f32[16,72,128]{2,1,0:T(8,128)} %shard_map.39), calls=%async_computation.2 | async-start | bytes 1179648 | tf_op jit(solution)/shard_map/all_to_all | solution.py:449
  51.2 13.9 %collective-permute-start.1 = (f32[32,8,128]{2,1,0:T(8,128)S(1)}, f32[32,8,128]{2,1,0:T(8,128)S(1)}, u32[]{:S(2)}, u32[]{:S(2)}) collective-permute-start(f32[32,8,128]{2,1,0:T(8,128)S(1)} %get-tuple-element.10), channel_id=1, source_target_pairs={{64,128},{192,256},{320,384},{128,64},{256,192},{384,320},{65,129}... | collective-permute-start | bytes 393224 | tf_op jit(solution)/shard_map/ppermute | solution.py:432
  58.9 8.1 %collective-permute-start = (f32[32,8,128]{2,1,0:T(8,128)S(1)}, f32[32,8,128]{2,1,0:T(8,128)S(1)}, u32[]{:S(2)}, u32[]{:S(2)}) collective-permute-start(f32[32,8,128]{2,1,0:T(8,128)S(1)} %get-tuple-element.9), channel_id=1, source_target_pairs={{0,64},{64,0},{1,65},{65,1},{2,66},{66,2},{3,67},{67,3},{4,68},{68... | collective-permute-start | bytes 393224 | tf_op jit(solution)/shard_map/ppermute | solution.py:427
  65.1 7.0 %collective-permute-start.2 = (f32[32,8,128]{2,1,0:T(8,128)S(1)}, f32[32,8,128]{2,1,0:T(8,128)S(1)}, u32[]{:S(2)}, u32[]{:S(2)}) collective-permute-start(f32[32,8,128]{2,1,0:T(8,128)S(1)} %collective-permute-done.1.outer1_ref), channel_id=1, source_target_pairs={{0,64},{64,0},{1,65},{65,1},{2,66},{66,2},{3,67},{67,3},{4,68},{68... | collective-permute-start | bytes 393224 | tf_op jit(solution)/shard_map/ppermute | solution.py:427
  67.0 12.8 %collective-permute-start.3 = (f32[32,8,128]{2,1,0:T(8,128)S(1)}, f32[32,8,128]{2,1,0:T(8,128)S(1)}, u32[]{:S(2)}, u32[]{:S(2)}) collective-permute-start(f32[32,8,128]{2,1,0:T(8,128)S(1)} %collective-permute-done.inner1_ref), channel_id=1, source_target_pairs={{64,128},{192,256},{320,384},{128,64},{256,192},{384,320},{65,129}... | collective-permute-start | bytes 393224 | tf_op jit(solution)/shard_map/ppermute | solution.py:432
